TPU v7x, 256 devices: a whole 4x4x8 slice. The times are simulated.
256 devices in a mesh: img: 8 (over x, y_lo), atom: 32 (over y_hi, z, core).
Axes of the slice: x: 4, y: 4 (y_hi: 2, y_lo: 2; y = y_hi * 2 + y_lo), z: 8, core: 2. Of those that a mesh axis runs over, the one named last changes fastest.
Arguments:
- positions: float32 [8, 3, 32768], P('img', None, 'atom'), may hold values from -14.6 to 14.6, as said below
- species: int32 [32768], P('atom'), may hold values from 0 to 3
- counts: int32 [32768], P('atom'), may hold values from 1 to 16, as said below
- neighbours: int32 [16, 32768], P(None, 'atom'), may hold values from 0 to 1535, as said below
- send_list: int32 [16384], P('atom'), may hold values from 0 to 1023
- climb: int32 [8], P('img'), may hold values 0 or 1
- embed: bfloat16 [4, 128], replicated, may hold values from -6 to 6
- ref_energy: float32 [4], replicated, may hold values from -2 to 2
- rad_in: bfloat16 [3, 8, 64], replicated, may hold values from -24 to 24
- rad_out: bfloat16 [3, 64, 128], replicated, may hold values from -0.047851562 to 0.047851562
- mixing: bfloat16 [2, 128, 128], replicated, may hold values from -0.5 to 0.5
- w_energy: bfloat16 [128], replicated, may hold values from -0.5 to 0.5
Outputs:
- neb_force: float32 [8, 3, 32768], P('img', None, 'atom')
- energies: float32 [8], P('img')
Inputs may be any that keep to these rules, and one draw needn't show every extreme that they name: `positions`: positions of image p are those of image 0 plus a sum of p random displacements. `counts`: the first atom of every tile has all 16 slots live. `neighbours`: every slot of the atom with local index i (its index mod 1024) names a row from i to i + 512 of its tile's table, never row i + 256. `send_list`: values are local atom indices of the owning tile.
All inputs are finite; a program needn't handle non-finite values. No bound on the sum of `climb` on one device may be relied on, other than what follows from the above.
Results may differ from a plain program's by a relative error of at most 0.007.
Values may be sent and summed in bfloat16 or wider, within the bound.
A program may use at most 64 MiB of HBM per device.

v0:
```python
import math

import jax
import jax.numpy as jnp
from jax import lax
from jax.sharding import PartitionSpec as P

spring_constant = 5.0


def padded(block, sides, width, periodic):
    for axis, dim in sides:
        count = lax.axis_size(axis)
        forward = [(i, i + 1) for i in range(count - 1)]
        if periodic:
            forward.append((count - 1, 0))
        backward = [(target, source) for source, target in forward]
        low = lax.ppermute(
            lax.slice_in_dim(block, block.shape[dim] - width, None, axis=dim), axis, forward
        )
        high = lax.ppermute(lax.slice_in_dim(block, 0, width, axis=dim), axis, backward)
        block = jnp.concatenate([low, block, high], axis=dim)
    return block


def radial_field(basis, w_in, w_out):
    hidden = lax.dot_general(
        w_in, basis, (((0,), (0,)), ((), ())), preferred_element_type=jnp.float32
    )
    hidden = jax.nn.silu(hidden).astype(jnp.bfloat16)
    return lax.dot_general(
        hidden, w_out, (((0,), (0,)), ((), ())), preferred_element_type=jnp.float32
    )


def species_table(kinds, embed):
    onehot = (kinds[:, None] == jnp.arange(embed.shape[0], dtype=jnp.int32)[None, :]).astype(
        jnp.bfloat16
    )
    return jnp.dot(onehot, embed, preferred_element_type=jnp.float32).astype(jnp.bfloat16)


def feature_rim(feats, send_list, rim_rows):
    sent = jnp.take(feats, send_list, axis=0)
    rims = padded(sent, (("atom", 0),), rim_rows, True)
    return jnp.concatenate([rims[:rim_rows], feats, rims[3 * rim_rows :]], axis=0)


def to_blocks(arr, block):
    lead = arr.shape[:-1]
    number = arr.shape[-1] // block
    arr = arr.reshape(lead + (number, block))
    return jnp.moveaxis(arr, -2, 0)


def selector(nbr_b, start, window):
    local_rows = nbr_b - start
    columns = lax.broadcasted_iota(jnp.int32, (1, 1, window), 2)
    picks = local_rows[:, :, None] == columns
    return picks.reshape(nbr_b.shape[0] * nbr_b.shape[1], window)


def on_device(
    positions,
    species,
    counts,
    neighbours,
    send_list,
    climb,
    embed,
    ref_energy,
    rad_in,
    rad_out,
    mixing,
    w_energy,
):
    atoms = species.shape[0]
    rim_rows = send_list.shape[0] // 2
    fan = neighbours.shape[0]
    chans = embed.shape[1]
    layers = mixing.shape[0]
    basis_count = rad_in.shape[1]
    block = min(256, atoms)
    number = atoms // block
    window = block + 2 * rim_rows
    block_starts = jnp.arange(number, dtype=jnp.int32) * block
    here = positions[0]
    sent_pos = jnp.take(here, send_list, axis=1)
    rim_pos = padded(sent_pos, (("atom", 1),), rim_rows, True)
    table_pos = jnp.concatenate([rim_pos[:, :rim_rows], here, rim_pos[:, 3 * rim_rows :]], axis=1)
    nbr_blocks = to_blocks(neighbours, block)

    def locate(items):
        nbr_b, start = items
        near_pos = lax.dynamic_slice_in_dim(table_pos, start, window, 1)
        picks = selector(nbr_b, start, window).astype(jnp.float32)
        reached = lax.dot_general(
            near_pos,
            picks,
            (((1,), (1,)), ((), ())),
            precision=lax.Precision.HIGHEST,
            preferred_element_type=jnp.float32,
        )
        centre = lax.dynamic_slice_in_dim(here, start + rim_rows - rim_rows, block, 1)
        return reached.reshape(3, fan, block) - centre[:, None, :]

    delta_blocks = lax.map(locate, (nbr_blocks, block_starts))
    dist_sq = jnp.sum(delta_blocks * delta_blocks, axis=1)
    centres = 2.0 * jnp.arange(basis_count, dtype=jnp.float32)
    basis_blocks = jnp.exp(
        -jnp.square(dist_sq[:, None] - centres[None, :, None, None]) / 8.0
    ).astype(jnp.bfloat16)
    basis_blocks = basis_blocks.reshape(number, basis_count, fan * block)
    slots = lax.broadcasted_iota(jnp.int32, (fan, atoms), 0)
    live = (slots < counts[None, :]).astype(jnp.float32)
    live_blocks = to_blocks(live, block)
    own = species_table(species, embed)
    table_h = feature_rim(own, send_list, rim_rows)

    def fetch(table, nbr_b, start):
        near_rows = lax.dynamic_slice_in_dim(table, start, window, 0)
        picks = selector(nbr_b, start, window).astype(jnp.bfloat16)
        return jnp.dot(picks, near_rows, preferred_element_type=jnp.float32).reshape(
            fan, block, chans
        )

    feats = own
    for layer in range(layers):
        if layer > 0:
            table_h = feature_rim(feats, send_list, rim_rows)

        def step(items, table=table_h, layer=layer):
            nbr_b, start, basis_b, live_b, feats_b = items
            field = radial_field(basis_b, rad_in[layer], rad_out[layer]).reshape(fan, block, chans)
            far = fetch(table, nbr_b, start)
            summed = jnp.sum(field * far * live_b[:, :, None], axis=0)
            scaled = (summed / math.sqrt(fan)).astype(jnp.bfloat16)
            update = jax.nn.silu(jnp.dot(scaled, mixing[layer], preferred_element_type=jnp.float32))
            return (feats_b.astype(jnp.float32) + update).astype(jnp.bfloat16)

        feats = lax.map(
            step,
            (
                nbr_blocks,
                block_starts,
                basis_blocks,
                live_blocks,
                feats.reshape(number, block, chans),
            ),
        ).reshape(atoms, chans)
    table_h = feature_rim(feats, send_list, rim_rows)

    def force_step(items):
        nbr_b, start, basis_b, live_b, feats_b, delta_b = items
        field = radial_field(basis_b, rad_in[layers], rad_out[layers]).reshape(fan, block, chans)
        far = fetch(table_h, nbr_b, start)
        near = feats_b.astype(jnp.float32)[None]
        pair = jnp.sum(field * near * far, axis=2) * (live_b / math.sqrt(chans))
        return jnp.sum(pair[None] * delta_b, axis=1)

    force_blocks = lax.map(
        force_step,
        (
            nbr_blocks,
            block_starts,
            basis_blocks,
            live_blocks,
            feats.reshape(number, block, chans),
            delta_blocks,
        ),
    )
    force = jnp.moveaxis(force_blocks, 0, 1).reshape(3, atoms)
    onehot_ref = jnp.where(
        species[:, None] == jnp.arange(ref_energy.shape[0], dtype=jnp.int32)[None, :],
        ref_energy[None, :],
        jnp.float32(0.0),
    )
    per_atom = jnp.dot(feats, w_energy, preferred_element_type=jnp.float32) + jnp.sum(
        onehot_ref, axis=1
    )
    energy_part = jnp.sum(per_atom)
    band = padded(positions, (("img", 0),), 1, False)
    behind = here - band[0]
    ahead = band[2] - here
    energy_sum, back_sq, fore_sq = lax.psum(
        (energy_part, jnp.sum(behind * behind), jnp.sum(ahead * ahead)), "atom"
    )
    back_len = jnp.sqrt(back_sq + 1e-06)
    fore_len = jnp.sqrt(fore_sq + 1e-06)
    tangent = behind / back_len + ahead / fore_len
    tau_sq, along = lax.psum((jnp.sum(tangent * tangent), jnp.sum(force * tangent)), "atom")
    index = lax.axis_index("img")
    last = lax.axis_size("img") - 1
    proj = along / tau_sq
    interior = (
        force
        - proj * tangent
        + spring_constant * (fore_len - back_len) / jnp.sqrt(tau_sq) * tangent
    )
    climbing = force - 2.0 * proj * tangent
    is_end = jnp.logical_or(index == 0, index == last)
    result = jnp.where(is_end, force, jnp.where(climb[0] == 1, climbing, interior))
    energy = (energy_sum / (atoms * lax.axis_size("atom"))).reshape(1)
    return (result[None], energy)


def solution(mesh):
    return jax.shard_map(
        on_device,
        mesh=mesh,
        in_specs=(
            P("img", None, "atom"),
            P("atom"),
            P("atom"),
            P(None, "atom"),
            P("atom"),
            P("img"),
            P(),
            P(),
            P(),
            P(),
            P(),
            P(),
        ),
        out_specs=(P("img", None, "atom"), P("img")),
        check_vma=False,
    )
```

profile of v0, /device:TPU:6, one launch (start us, length us, event | category | flops | bytes accessed | tf_op | source)
XLA Modules:
  0.0 342.7 jit_solution(10693360866977747864)
XLA Ops:
  0.7 1.0 copy.71
  1.7 3.5 %collective-permute-start.8 = (f32[1,3,1024]{1,2,0:T(8,128)S(1)}, f32[1,3,1024]{1,2,0:T(8,128)S(1)}, u32[]{:S(2)}, u32[]{:S(2)}) collective-permute-start(f32[1,3,1024]{1,2,0:T(8,128)S(1)} %copy.71), channel_id=1, source_target_pairs={{0,32},{32,64},{64,96},{96,128},{128,160},{160,192},{192,224},{1,3... | collective-permute-start | bytes 36872 | tf_op jit(solution)/shard_map/ppermute | solution.py:18
  5.2 3.3 collective-permute-start.9
  9.8 1.0 gather_fusion
  11.1 7.4 %collective-permute-start.1 = (f32[3,256]{0,1:T(8,128)S(1)}, f32[3,256]{0,1:T(8,128)S(1)}, u32[]{:S(2)}, u32[]{:S(2)}) collective-permute-start(f32[3,256]{0,1:T(8,128)S(1)} %get-tuple-element.528), channel_id=1, source_target_pairs={{1,0},{2,1},{3,2},{4,3},{5,4},{6,5},{7,6},{8,7},{9,8},{10,9},{11,1... | collective-permute-start | bytes 9224 | tf_op jit(solution)/shard_map/ppermute | solution.py:21
  18.6 1.0 convolution_convert_fusion
  19.6 1.3 gather_fusion.1
  22.8 5.4 %collective-permute-start.3 = (bf16[256,128]{1,0:T(8,128)(2,1)}, bf16[256,128]{1,0:T(8,128)(2,1)S(1)}, u32[]{:S(2)}, u32[]{:S(2)}) collective-permute-start(bf16[256,128]{1,0:T(8,128)(2,1)} %get-tuple-element.534), channel_id=1, source_target_pairs={{1,0},{2,1},{3,2},{4,3},{5,4},{6,5},{7,6},{8,7},{9,8},{10,9},{11,1... | collective-permute-start | bytes 196616 | tf_op jit(solution)/shard_map/ppermute | solution.py:21
  28.4 41.1 %while.44 = (s32[]{:T(128)}, f32[4,3,16,256]{3,1,2,0:T(4,128)S(1)}, s32[4]{0:T(128)S(1)}, f32[3,1536]{1,0:T(4,128)S(1)}, s32[4,16,256]{2,1,0:T(8,128)S(1)}, /*in...) while((s32[]{:T(128)}, f32[4,3,16,256]{3,1,2,0:T(4,128)S(1)}, s32[4]{0:T(128)S(1)}, ...), condition=%wide.region_1.2_spmd, body=%wide.region_0.1_spmd.sunk | while | flops 116408328 | bytes 137408 | solution.py:107
  32.5 6.2 %fusion.110 = f32[4,3,16,256]{3,1,2,0:T(4,128)S(1)} fusion(f32[4,3,16,256]{3,1,2,0:T(4,128)S(1)} %get-tuple-element.784, s32[]{:T(128)} %get-tuple-element.783, s32[16,256]{1,0:T(8,128)S(1)} %subtract_bitcast_fusion.8, f32[3,256]{1,0:T(4,128)S(1)} %constant_dynamic-slice_fusion.4, f32[3,1536]{1,0:T(4,128)S(1)} %get-tuple-element.796, s32[]{:T(128)S(6)} %select_n.100), kind=kOutput, calls=%fused_computation.9.clone.1 | convolution fusion | flops 116404224 | bytes 98312 | tf_op jit(solution)/shard_map/while/body/eval_jaxpr/dot_general | solution.py:97
  42.8 6.2 %fusion.110 = f32[4,3,16,256]{3,1,2,0:T(4,128)S(1)} fusion(f32[4,3,16,256]{3,1,2,0:T(4,128)S(1)} %get-tuple-element.784, s32[]{:T(128)} %get-tuple-element.783, s32[16,256]{1,0:T(8,128)S(1)} %subtract_bitcast_fusion.8, f32[3,256]{1,0:T(4,128)S(1)} %constant_dynamic-slice_fusion.4, f32[3,1536]{1,0:T(4,128)S(1)} %get-tuple-element.796, s32[]{:T(128)S(6)} %select_n.100), kind=kOutput, calls=%fused_computation.9.clone.1 | convolution fusion | flops 116404224 | bytes 98312 | tf_op jit(solution)/shard_map/while/body/eval_jaxpr/dot_general | solution.py:97
  53.0 6.2 %fusion.110 = f32[4,3,16,256]{3,1,2,0:T(4,128)S(1)} fusion(f32[4,3,16,256]{3,1,2,0:T(4,128)S(1)} %get-tuple-element.784, s32[]{:T(128)} %get-tuple-element.783, s32[16,256]{1,0:T(8,128)S(1)} %subtract_bitcast_fusion.8, f32[3,256]{1,0:T(4,128)S(1)} %constant_dynamic-slice_fusion.4, f32[3,1536]{1,0:T(4,128)S(1)} %get-tuple-element.796, s32[]{:T(128)S(6)} %select_n.100), kind=kOutput, calls=%fused_computation.9.clone.1 | convolution fusion | flops 116404224 | bytes 98312 | tf_op jit(solution)/shard_map/while/body/eval_jaxpr/dot_general | solution.py:97
  63.3 6.2 %fusion.110 = f32[4,3,16,256]{3,1,2,0:T(4,128)S(1)} fusion(f32[4,3,16,256]{3,1,2,0:T(4,128)S(1)} %get-tuple-element.784, s32[]{:T(128)} %get-tuple-element.783, s32[16,256]{1,0:T(8,128)S(1)} %subtract_bitcast_fusion.8, f32[3,256]{1,0:T(4,128)S(1)} %constant_dynamic-slice_fusion.4, f32[3,1536]{1,0:T(4,128)S(1)} %get-tuple-element.796, s32[]{:T(128)S(6)} %select_n.100), kind=kOutput, calls=%fused_computation.9.clone.1 | convolution fusion | flops 116404224 | bytes 98312 | tf_op jit(solution)/shard_map/while/body/eval_jaxpr/dot_general | solution.py:97
  71.6 65.6 %all-reduce.1 = (f32[]{:T(128)}, f32[]{:T(128)}) all-reduce(f32[]{:T(128)} %get-tuple-element.443, f32[]{:T(128)} %get-tuple-element.442), channel_id=1, replica_groups=mesh['img'=8,'atom'=32] {'atom'}, use_global_device_ids=true, to_apply=%region_16.18 | all-reduce | flops 2 | bytes 16 | tf_op jit(solution)/shard_map/psum | solution.py:185
  139.4 35.2 %while.45 = (s32[]{:T(128)}, bf16[4,256,128]{2,1,0:T(8,128)(2,1)S(1)}, bf16[4,256,128]{2,1,0:T(8,128)(2,1)S(1)}, bf16[4,8,4096]{2,1,0:T(8,128)(2,1)}, bf16[3,8,6...) while((s32[]{:T(128)}, ...), condition=%wide.region_5.7_spmd, body=%wide.region_3.6_spmd.sunk | while | flops 891293696 | bytes 7621347 | solution.py:141
  142.6 1.3 multiply_convert_fusion.25
  145.0 3.1 multiply_reduce_fusion.11
  151.4 1.3 multiply_convert_fusion.25
  153.8 3.0 multiply_reduce_fusion.11
  160.2 1.3 multiply_convert_fusion.25
  162.6 3.0 multiply_reduce_fusion.11
  169.1 1.3 multiply_convert_fusion.25
  171.4 3.0 multiply_reduce_fusion.11
  174.7 1.3 gather_fusion.2
  176.3 5.3 %collective-permute-start.5 = (bf16[256,128]{1,0:T(8,128)(2,1)S(1)}, bf16[256,128]{1,0:T(8,128)(2,1)S(1)}, u32[]{:S(2)}, u32[]{:S(2)}) collective-permute-start(bf16[256,128]{1,0:T(8,128)(2,1)S(1)} %get-tuple-element.532), channel_id=1, source_target_pairs={{1,0},{2,1},{3,2},{4,3},{5,4},{6,5},{7,6},{8,7},{9,8},{10,9},{11,1... | collective-permute-start | bytes 196616 | tf_op jit(solution)/shard_map/ppermute | solution.py:21
  182.6 1.0 collective-permute-done.4
  183.6 33.3 %while.46 = (s32[]{:T(128)}, bf16[4,256,128]{2,1,0:T(8,128)(2,1)S(1)}, bf16[4,256,128]{2,1,0:T(8,128)(2,1)S(1)}, bf16[4,8,4096]{2,1,0:T(8,128)(2,1)}, bf16[3,8,6...) while((s32[]{:T(128)}, ...), condition=%wide.region_8.10_spmd, body=%wide.region_6.9_spmd.sunk | while | flops 891293696 | bytes 6048455 | solution.py:141
  186.8 1.3 multiply_convert_fusion.27
  188.7 3.1 multiply_reduce_fusion.12
  195.2 1.3 multiply_convert_fusion.27
  197.0 3.1 multiply_reduce_fusion.12
  203.5 1.3 multiply_convert_fusion.27
  205.3 3.1 multiply_reduce_fusion.12
  211.8 1.3 multiply_convert_fusion.27
  213.6 3.1 multiply_reduce_fusion.12
  217.4 1.3 gather_fusion.3
  219.0 5.4 %collective-permute-start.7 = (bf16[256,128]{1,0:T(8,128)(2,1)S(1)}, bf16[256,128]{1,0:T(8,128)(2,1)S(1)}, u32[]{:S(2)}, u32[]{:S(2)}) collective-permute-start(bf16[256,128]{1,0:T(8,128)(2,1)S(1)} %get-tuple-element.530), channel_id=1, source_target_pairs={{1,0},{2,1},{3,2},{4,3},{5,4},{6,5},{7,6},{8,7},{9,8},{10,9},{11,1... | collective-permute-start | bytes 196616 | tf_op jit(solution)/shard_map/ppermute | solution.py:21
  225.3 1.0 collective-permute-done.6
  227.1 38.9 %while.47 = (s32[]{:T(128)}, f32[4,3,256]{2,1,0:T(4,128)S(1)}, bf16[4,8,4096]{2,1,0:T(8,128)(2,1)}, bf16[3,8,64]{2,1,0:T(8,128)(2,1)}, bf16[3,64,128]{2,1,0:T(8,...) while((s32[]{:T(128)}, f32[4,3,256]{2,1,0:T(4,128)S(1)}, ...), condition=%wide.region_12.14_spmd, body=%wide.region_9.13_spmd.sunk | while | flops 882703616 | bytes 6305487 | solution.py:161
  230.3 1.3 multiply_convert_fusion.28
  232.3 4.5 %multiply_reduce_fusion.13 = f32[16,256]{1,0:T(8,128)S(1)} fusion(f32[16,256,128]{1,2,0:T(8,128)S(1)} %fusion.132, s32[16,256]{1,0:T(8,128)S(1)} %subtract_bitcast_fusion.11, f32[256,128]{0,1:T(8,128)S(1)} %bitcast_convert_fusion.2, bf16[1536,128]{1,0:T(8,128)(2,1)} %get-tuple-element.923, s32[]{:T(128)S(6)} %select_n.103), kind=kOutput, calls=%fused_computation.78.clone.1 | convolution fusion | flops 810020864 | bytes 2457604 | tf_op jit(solution)/shard_map/while/body/eval_jaxpr/dot_general | solution.py:123
  240.0 1.3 multiply_convert_fusion.28
  242.0 4.5 %multiply_reduce_fusion.13 = f32[16,256]{1,0:T(8,128)S(1)} fusion(f32[16,256,128]{1,2,0:T(8,128)S(1)} %fusion.132, s32[16,256]{1,0:T(8,128)S(1)} %subtract_bitcast_fusion.11, f32[256,128]{0,1:T(8,128)S(1)} %bitcast_convert_fusion.2, bf16[1536,128]{1,0:T(8,128)(2,1)} %get-tuple-element.923, s32[]{:T(128)S(6)} %select_n.103), kind=kOutput, calls=%fused_computation.78.clone.1 | convolution fusion | flops 810020864 | bytes 2457604 | tf_op jit(solution)/shard_map/while/body/eval_jaxpr/dot_general | solution.py:123
  249.8 1.3 multiply_convert_fusion.28
  251.7 4.5 %multiply_reduce_fusion.13 = f32[16,256]{1,0:T(8,128)S(1)} fusion(f32[16,256,128]{1,2,0:T(8,128)S(1)} %fusion.132, s32[16,256]{1,0:T(8,128)S(1)} %subtract_bitcast_fusion.11, f32[256,128]{0,1:T(8,128)S(1)} %bitcast_convert_fusion.2, bf16[1536,128]{1,0:T(8,128)(2,1)} %get-tuple-element.923, s32[]{:T(128)S(6)} %select_n.103), kind=kOutput, calls=%fused_computation.78.clone.1 | convolution fusion | flops 810020864 | bytes 2457604 | tf_op jit(solution)/shard_map/while/body/eval_jaxpr/dot_general | solution.py:123
  259.5 1.3 multiply_convert_fusion.28
  261.5 4.5 %multiply_reduce_fusion.13 = f32[16,256]{1,0:T(8,128)S(1)} fusion(f32[16,256,128]{1,2,0:T(8,128)S(1)} %fusion.132, s32[16,256]{1,0:T(8,128)S(1)} %subtract_bitcast_fusion.11, f32[256,128]{0,1:T(8,128)S(1)} %bitcast_convert_fusion.2, bf16[1536,128]{1,0:T(8,128)(2,1)} %get-tuple-element.923, s32[]{:T(128)S(6)} %select_n.103), kind=kOutput, calls=%fused_computation.78.clone.1 | convolution fusion | flops 810020864 | bytes 2457604 | tf_op jit(solution)/shard_map/while/body/eval_jaxpr/dot_general | solution.py:123
  266.6 71.1 %all-reduce = (f32[]{:T(128)}, f32[]{:T(128)}, f32[]{:T(128)}) all-reduce(f32[]{:T(128)} %multiply_reduce_fusion.3, f32[]{:T(128)} %multiply_reduce_fusion.7, f32[]{:T(128)} %add_reduce_fusion), channel_id=1, replica_groups=mesh['img'=8,'atom'=32] {'atom'}, use_global_device_ids=true, to_apply=%region_20.22 | all-reduce | flops 3 | bytes 24 | tf_op jit(solution)/shard_map/psum | solution.py:191
  (175 shorter events, 41.2 us)
Async XLA Ops:
  0.6 17.9 %copy-start = (bf16[4,128]{1,0:T(4,128)(2,1)S(1)}, bf16[4,128]{1,0:T(4,128)(2,1)}, u32[]{:S(2)}) copy-start(bf16[4,128]{1,0:T(4,128)(2,1)} %param.28) | copy-start | bytes 3076
  0.6 21.1 %copy-start.4 = (s32[1024]{0:T(1024)S(1)}, s32[1024]{0:T(1024)}, u32[]{:S(2)}) copy-start(s32[1024]{0:T(1024)} %param.23) | copy-start | bytes 12292
  0.7 21.1 %copy-start.5 = (s32[1024]{0:T(1024)S(1)}, s32[1024]{0:T(1024)}, u32[]{:S(2)}) copy-start(s32[1024]{0:T(1024)} %param.24) | copy-start | bytes 12292
  0.7 21.1 %copy-start.7 = (f32[4]{0:T(128)S(1)}, f32[4]{0:T(128)}, u32[]{:S(2)}) copy-start(f32[4]{0:T(128)} %param.29) | copy-start | bytes 52
  0.7 21.4 %copy-start.3 = (s32[16,1024]{1,0:T(8,128)S(1)}, s32[16,1024]{1,0:T(8,128)}, u32[]{:S(2)}) copy-start(s32[16,1024]{1,0:T(8,128)} %param.25) | copy-start | bytes 196612
  1.7 69.0 %collective-permute-start.8 = (f32[1,3,1024]{1,2,0:T(8,128)S(1)}, f32[1,3,1024]{1,2,0:T(8,128)S(1)}, u32[]{:S(2)}, u32[]{:S(2)}) collective-permute-start(f32[1,3,1024]{1,2,0:T(8,128)S(1)} %copy.71), channel_id=1, source_target_pairs={{0,32},{32,64},{64,96},{96,128},{128,160},{160,192},{192,224},{1,3... | collective-permute-start | bytes 36872 | tf_op jit(solution)/shard_map/ppermute | solution.py:18
  5.2 65.5 %collective-permute-start.9 = (f32[1,3,1024]{1,2,0:T(8,128)S(1)}, f32[1,3,1024]{1,2,0:T(8,128)S(1)}, u32[]{:S(2)}, u32[]{:S(2)}) collective-permute-start(f32[1,3,1024]{1,2,0:T(8,128)S(1)} %copy.71), channel_id=1, source_target_pairs={{32,0},{64,32},{96,64},{128,96},{160,128},{192,160},{224,192},{33,... | collective-permute-start | bytes 36872 | tf_op jit(solution)/shard_map/ppermute | solution.py:21
  11.0 11.8 %collective-permute-start = (f32[3,256]{0,1:T(8,128)S(1)}, f32[3,256]{0,1:T(8,128)S(1)}, u32[]{:S(2)}, u32[]{:S(2)}) collective-permute-start(f32[3,256]{0,1:T(8,128)S(1)} %get-tuple-element.527), channel_id=1, source_target_pairs={{0,1},{1,2},{2,3},{3,4},{4,5},{5,6},{6,7},{7,8},{8,9},{9,10},{10,1... | collective-permute-start | bytes 9224 | tf_op jit(solution)/shard_map/ppermute | solution.py:18
  11.1 17.2 %collective-permute-start.1 = (f32[3,256]{0,1:T(8,128)S(1)}, f32[3,256]{0,1:T(8,128)S(1)}, u32[]{:S(2)}, u32[]{:S(2)}) collective-permute-start(f32[3,256]{0,1:T(8,128)S(1)} %get-tuple-element.528), channel_id=1, source_target_pairs={{1,0},{2,1},{3,2},{4,3},{5,4},{6,5},{7,6},{8,7},{9,8},{10,9},{11,1... | collective-permute-start | bytes 9224 | tf_op jit(solution)/shard_map/ppermute | solution.py:21
  21.7 116.8 %collective-permute-start.2 = (bf16[256,128]{1,0:T(8,128)(2,1)}, bf16[256,128]{1,0:T(8,128)(2,1)S(1)}, u32[]{:S(2)}, u32[]{:S(2)}) collective-permute-start(bf16[256,128]{1,0:T(8,128)(2,1)} %get-tuple-element.533), channel_id=1, source_target_pairs={{0,1},{1,2},{2,3},{3,4},{4,5},{5,6},{6,7},{7,8},{8,9},{9,10},{10,1... | collective-permute-start | bytes 196616 | tf_op jit(solution)/shard_map/ppermute | solution.py:18
  22.8 115.8 %collective-permute-start.3 = (bf16[256,128]{1,0:T(8,128)(2,1)}, bf16[256,128]{1,0:T(8,128)(2,1)S(1)}, u32[]{:S(2)}, u32[]{:S(2)}) collective-permute-start(bf16[256,128]{1,0:T(8,128)(2,1)} %get-tuple-element.534), channel_id=1, source_target_pairs={{1,0},{2,1},{3,2},{4,3},{5,4},{6,5},{7,6},{8,7},{9,8},{10,9},{11,1... | collective-permute-start | bytes 196616 | tf_op jit(solution)/shard_map/ppermute | solution.py:21
  69.5 1.1 copy-start.9
  70.6 68.8 %copy-start.1 = (bf16[3,64,128]{2,1,0:T(8,128)(2,1)S(1)}, bf16[3,64,128]{2,1,0:T(8,128)(2,1)}, u32[]{:S(2)}) copy-start(bf16[3,64,128]{2,1,0:T(8,128)(2,1)} %param.31) | copy-start | bytes 147460
  70.7 68.8 %copy-start.8 = (bf16[2,128,128]{2,1,0:T(8,128)(2,1)S(1)}, bf16[2,128,128]{2,1,0:T(8,128)(2,1)}, u32[]{:S(2)}) copy-start(bf16[2,128,128]{2,1,0:T(8,128)(2,1)} %param.32) | copy-start | bytes 196612
  70.7 68.8 %copy-start.10 = (s32[4]{0:T(128)S(1)}, s32[4]{0:T(128)}, u32[]{:S(2)}) copy-start(s32[4]{0:T(128)} %copy-done.9) | copy-start | bytes 52
  144.0 1.0 copy-start.2
  152.8 1.0 copy-start.2
  161.6 1.0 copy-start.2
  170.4 1.0 copy-start.2
  176.2 7.4 %collective-permute-start.4 = (bf16[256,128]{1,0:T(8,128)(2,1)S(1)}, bf16[256,128]{1,0:T(8,128)(2,1)S(1)}, u32[]{:S(2)}, u32[]{:S(2)}) collective-permute-start(bf16[256,128]{1,0:T(8,128)(2,1)S(1)} %get-tuple-element.531), channel_id=1, source_target_pairs={{0,1},{1,2},{2,3},{3,4},{4,5},{5,6},{6,7},{7,8},{8,9},{9,10},{10,1... | collective-permute-start | bytes 196616 | tf_op jit(solution)/shard_map/ppermute | solution.py:18
  176.3 7.3 %collective-permute-start.5 = (bf16[256,128]{1,0:T(8,128)(2,1)S(1)}, bf16[256,128]{1,0:T(8,128)(2,1)S(1)}, u32[]{:S(2)}, u32[]{:S(2)}) collective-permute-start(bf16[256,128]{1,0:T(8,128)(2,1)S(1)} %get-tuple-element.532), channel_id=1, source_target_pairs={{1,0},{2,1},{3,2},{4,3},{5,4},{6,5},{7,6},{8,7},{9,8},{10,9},{11,1... | collective-permute-start | bytes 196616 | tf_op jit(solution)/shard_map/ppermute | solution.py:21
  183.6 40.8 %copy-start.6 = (bf16[128]{0:T(256)(128)(2,1)S(1)}, bf16[128]{0:T(256)(128)(2,1)}, u32[]{:S(2)}) copy-start(bf16[128]{0:T(256)(128)(2,1)} %param.33) | copy-start | bytes 772
  216.9 0.5 copy-start.11
  217.4 9.7 %copy-start.12 = (s32[4]{0:T(128)S(1)}, s32[4]{0:T(128)}, u32[]{:S(2)}) copy-start(s32[4]{0:T(128)} %copy-done.11) | copy-start | bytes 52
  218.9 7.4 %collective-permute-start.6 = (bf16[256,128]{1,0:T(8,128)(2,1)S(1)}, bf16[256,128]{1,0:T(8,128)(2,1)S(1)}, u32[]{:S(2)}, u32[]{:S(2)}) collective-permute-start(bf16[256,128]{1,0:T(8,128)(2,1)S(1)} %get-tuple-element.529), channel_id=1, source_target_pairs={{0,1},{1,2},{2,3},{3,4},{4,5},{5,6},{6,7},{7,8},{8,9},{9,10},{10,1... | collective-permute-start | bytes 196616 | tf_op jit(solution)/shard_map/ppermute | solution.py:18
  219.0 7.3 %collective-permute-start.7 = (bf16[256,128]{1,0:T(8,128)(2,1)S(1)}, bf16[256,128]{1,0:T(8,128)(2,1)S(1)}, u32[]{:S(2)}, u32[]{:S(2)}) collective-permute-start(bf16[256,128]{1,0:T(8,128)(2,1)S(1)} %get-tuple-element.530), channel_id=1, source_target_pairs={{1,0},{2,1},{3,2},{4,3},{5,4},{6,5},{7,6},{8,7},{9,8},{10,9},{11,1... | collective-permute-start | bytes 196616 | tf_op jit(solution)/shard_map/ppermute | solution.py:21
where the time goes:
time: 344 us; the launch traced here: 343 us
  blocking collectives  137 us (40%)
  matrix products  91.6 us (27%)
  loops' own time  35.4 us (10%)
  starting transfers between devices  30.6 us (9%)
  local copies, waits for them, and re-layouts  21.3 us (6%)
  other arithmetic  18.1 us (5%)
  between operations  6.87 us (2%)
    psum x1, blocking collectives, on_device(): lax.psum((jnp.sum(tangent * tangent), jnp.sum(force * tangent)), 'atom')  71.1 us
    psum x1, blocking collectives, on_device(): lax.psum((energy_part, jnp.sum(behind * behind), jnp.sum(ahead * ahead)),...  65.6 us
    dot_general x12, matrix products, fetch(): jnp.dot(picks, near_rows, preferred_element_type=jnp.float32)  42.3 us
    ppermute x5, starting transfers between devices, padded(): lax.ppermute(lax.slice_in_dim(block, 0, width, axis=dim), axis, backward)  26.9 us
    dot_general x4, matrix products, locate(): lax.dot_general(near_pos, picks, (((1,), (1,)), ((), ())), precision=lax....  24.8 us
    another operation x2, loops' own time, on_device(): lax.map(step, (nbr_blocks, block_starts, basis_blocks, live_blocks, feats...  16 us
    dot_general x12, matrix products, radial_field(): lax.dot_general(w_in, basis, (((0,), (0,)), ((), ())), preferred_element_...  15.9 us
    another operation x1, loops' own time, on_device(): delta_blocks = lax.map(locate, (nbr_blocks, block_starts))  11.3 us
  transfers between devices with their start and end apart: 10, of which 2 were waited for; matrix products, arithmetic and copies ran while one was open for 12% of the time, Pallas kernels for 0%

commit v1 on v0

v1 whole, which is shorter than its diff:
```python
import functools
import math

import jax
import jax.numpy as jnp
from jax import lax
from jax.experimental import pallas as pl
from jax.experimental.pallas import tpu as pltpu
from jax.sharding import PartitionSpec as P

F32 = jnp.float32
BF16 = jnp.bfloat16
I32 = jnp.int32
MESH = pl.DeviceIdType.MESH

SPRING = 5.0
C = 128
RAD = 64
NB = 8
SPECIES = 4
FAN = 16
HALO = 256
ATOMS = 1024
BLK = 256
BLOCKS = ATOMS // BLK
WIN = BLK + 2 * HALO
TABLE = ATOMS + 2 * HALO
LANES = 128
FAR_AWAY = 1.0e4


def lane_gather(source, index):
    return jnp.take_along_axis(source, index, axis=1, mode="promise_in_bounds")


def dot(a, b):
    return jnp.dot(a, b, preferred_element_type=F32)


def total(x):
    return jnp.sum(jnp.sum(x, axis=0, keepdims=True), axis=1, keepdims=True)


def one_hot_rows(index, tile, iota):
    local = index - float(256 * tile)
    inside = jnp.logical_and(local >= 0.0, local < 256.0)
    local = jnp.where(inside, local, -1.0)
    local = jnp.broadcast_to(local, (16, local.shape[1])).astype(BF16)
    local = jnp.concatenate([local] * 16, axis=0)
    return jnp.where(local == iota, jnp.ones_like(iota), jnp.zeros_like(iota))


def kernel(
    n_img,
    n_atom,
    pos,
    species,
    counts,
    neighbours,
    send_list,
    climb,
    embed,
    ref_energy,
    rad_in,
    rad_out,
    mixing,
    w_energy,
    out,
    energy_out,
    ptab,
    sendpos,
    band,
    t1,
    t2,
    sendh,
    onehot,
    sendhot,
    iota_ref,
    hid,
    masked,
    w_hid,
    w_first,
    rad_t,
    mix_t,
    emb_t,
    basis,
    sp_mask,
    sp_far,
    delta,
    force,
    rbuf,
    pos_send,
    pos_recv,
    img_send,
    img_recv,
    h_send,
    h_recv,
    r_send,
    r_recv,
):
    img = lax.axis_index("img")
    me = lax.axis_index("atom")
    up = lax.rem(me + 1, n_atom)
    down = lax.rem(me + n_atom - 1, n_atom)
    img_up = lax.rem(img + 1, n_img)
    img_down = lax.rem(img + n_img - 1, n_img)

    barrier = pltpu.get_barrier_semaphore()

    def greet(d, _):
        peer = lax.rem(me + d, n_atom)
        pl.semaphore_signal(barrier, inc=1, device_id=(img, peer), device_id_type=MESH)
        return 0

    lax.fori_loop(1, n_atom, greet, 0)
    for other in (img_up, img_down):
        pl.semaphore_signal(barrier, inc=1, device_id=(other, me), device_id_type=MESH)

    ptab[0:3, HALO : HALO + ATOMS] = pos[0]
    ptab[3:4, HALO : HALO + ATOMS] = species[...].astype(F32)
    ptab[4:8, HALO : HALO + ATOMS] = jnp.zeros((4, ATOMS), F32)
    for t in range(4):
        index = jnp.broadcast_to(send_list[:, t * LANES : (t + 1) * LANES], (8, LANES))
        low = index & 127
        high = index >> 7
        got = jnp.zeros((8, LANES), F32)
        for w in range(ATOMS // LANES):
            source = ptab[:, HALO + w * LANES : HALO + (w + 1) * LANES]
            got = jnp.where(high == w, lane_gather(source, low), got)
        sendpos[:, t * LANES : (t + 1) * LANES] = got

    row = lax.broadcasted_iota(I32, (256, BLK), 0).astype(F32).astype(BF16)
    iota_ref[...] = row
    for layer in range(3):
        rad_t[layer] = rad_out[layer].astype(F32).T.astype(BF16)
    for layer in range(2):
        mix_t[layer] = mixing[layer].astype(F32).T.astype(BF16)
    emb = embed[...].astype(F32)
    emb_rows = jnp.concatenate([emb, jnp.zeros((C - SPECIES, C), F32)], axis=0)
    emb_t[...] = emb_rows.T.astype(BF16)
    first = rad_out[0].astype(F32)
    w0 = jnp.concatenate([first * emb[k : k + 1, :] for k in range(SPECIES)], axis=0).T.astype(BF16)
    for s in range(FAN):
        w_first[:, s * 256 : (s + 1) * 256] = w0
    lane = lax.broadcasted_iota(I32, (NB, C), 1)
    spread = (lane // FAN == lax.broadcasted_iota(I32, (NB, C), 0)).astype(F32).astype(BF16)
    lane64 = lax.broadcasted_iota(I32, (RAD, C), 1) % FAN
    for layer in range(3):
        wide = lax.dot_general(
            rad_in[layer], spread, (((0,), (0,)), ((), ())), preferred_element_type=F32
        )
        wide = wide * 0.5
        for s in range(FAN):
            start = s * 192 + layer * RAD
            w_hid[start : start + RAD, :] = jnp.where(lane64 == s, wide, 0.0).astype(BF16)

    def send_row(t, slot, target):
        return pltpu.make_async_remote_copy(
            src_ref=t[0],
            dst_ref=t[1],
            send_sem=t[2].at[slot],
            recv_sem=t[3].at[slot],
            device_id=target,
            device_id_type=MESH,
        )

    def pos_copies():
        return (
            send_row(
                (sendpos.at[:, 0:HALO], ptab.at[:, HALO + ATOMS : TABLE], pos_send, pos_recv),
                0,
                (img, down),
            ),
            send_row(
                (sendpos.at[:, HALO : 2 * HALO], ptab.at[:, 0:HALO], pos_send, pos_recv),
                1,
                (img, up),
            ),
        )

    def img_copies():
        return (
            send_row((pos.at[0], band.at[0], img_send, img_recv), 0, (img_up, me)),
            send_row((pos.at[0], band.at[1], img_send, img_recv), 1, (img_down, me)),
        )

    def h_copies(phase, table):
        return (
            send_row(
                (
                    sendh.at[phase, :, 0:HALO],
                    table.at[:, HALO + ATOMS : TABLE],
                    h_send.at[phase],
                    h_recv.at[phase],
                ),
                0,
                (img, down),
            ),
            send_row(
                (
                    sendh.at[phase, :, HALO : 2 * HALO],
                    table.at[:, 0:HALO],
                    h_send.at[phase],
                    h_recv.at[phase],
                ),
                1,
                (img, up),
            ),
        )

    lane_row = lax.broadcasted_iota(I32, (1, LANES), 1)

    def reduce_start(phase, values):
        message = jnp.zeros((1, LANES), F32)
        for n, value in enumerate(values):
            message = jnp.where(lane_row == n, value, message)
        rbuf[phase, me] = message

        def each(d, _):
            peer = lax.rem(me + d, n_atom)
            pltpu.make_async_remote_copy(
                src_ref=rbuf.at[phase, me],
                dst_ref=rbuf.at[phase, me],
                send_sem=r_send.at[phase, peer],
                recv_sem=r_recv.at[phase, me],
                device_id=(img, peer),
                device_id_type=MESH,
            ).start()
            return 0

        lax.fori_loop(1, n_atom, each, 0)

    def reduce_wait(phase, number):
        def each(d, _):
            peer = lax.rem(me + d, n_atom)
            copy = pltpu.make_async_remote_copy(
                src_ref=rbuf.at[phase, me],
                dst_ref=rbuf.at[phase, peer],
                send_sem=r_send.at[phase, peer],
                recv_sem=r_recv.at[phase, peer],
                device_id=(img, peer),
                device_id_type=MESH,
            )
            copy.wait_send()
            copy.wait_recv()
            return 0

        lax.fori_loop(1, n_atom, each, 0)
        summed = jnp.sum(rbuf[phase], axis=0)
        return [
            jnp.sum(jnp.where(lane_row == n, summed, 0.0), axis=1, keepdims=True)
            for n in range(number)
        ]

    def order(i):
        return lax.rem(i + 1, BLOCKS)

    def first_block(i, _):
        block = order(i)
        start = pl.multiple_of(block * BLK, BLK)

        @pl.when(i == 1)
        def _():
            pl.semaphore_wait(barrier, n_atom + 1)
            for copy in pos_copies() + img_copies():
                copy.start()

        @pl.when(i == 2)
        def _():
            for copy in pos_copies() + img_copies():
                copy.wait()
            here = pos[0]
            behind = here - band[0]
            ahead = band[1] - here
            reduce_start(0, (total(behind * behind), total(ahead * ahead)))

        for t in range(BLK // LANES):
            at = pl.multiple_of(start + t * LANES, LANES)
            offset = neighbours[:, pl.ds(at, LANES)] - at
            low = offset & 127
            high = offset >> 7
            got = [None] * 4
            for w in range(WIN // LANES - 1):
                for comp in range(4):
                    source = jnp.broadcast_to(
                        ptab[comp : comp + 1, pl.ds(pl.multiple_of(at + w * LANES, LANES), LANES)],
                        (FAN, LANES),
                    )
                    value = lane_gather(source, low)
                    got[comp] = value if w == 0 else jnp.where(high == w, value, got[comp])
            slots = lax.broadcasted_iota(I32, (FAN, LANES), 0)
            live = slots < counts[:, pl.ds(at, LANES)]
            dist = jnp.zeros((FAN, LANES), F32)
            for comp in range(3):
                diff = got[comp] - pos[0, comp : comp + 1, pl.ds(at, LANES)]
                delta[comp, :, pl.ds(at, LANES)] = diff
                dist = dist + diff * diff
            dist = jnp.where(live, dist, FAR_AWAY)
            for k in range(NB):
                shifted = dist - 2.0 * k
                basis[k * FAN : (k + 1) * FAN, t * LANES : (t + 1) * LANES] = jnp.exp(
                    -(shifted * shifted) / 8.0
                ).astype(BF16)
            for k in range(SPECIES):
                sp_mask[k, :, t * LANES : (t + 1) * LANES] = (got[3] == float(k)).astype(F32)

        def slot(s, _):
            rows = pl.multiple_of(s * 192, 192)
            half = dot(w_hid[pl.ds(rows, 192), :], basis[...])
            unit = (half + half * jnp.tanh(half)).astype(BF16)
            at_row = pl.multiple_of(s * RAD, RAD)
            for layer in (1, 2):
                hid[layer - 1, pl.ds(at_row, RAD), pl.ds(start, BLK)] = unit[
                    layer * RAD : (layer + 1) * RAD
                ]
            for k in range(SPECIES):
                mask = jnp.broadcast_to(sp_mask[k, pl.ds(s, 1), :], (16, BLK)).astype(BF16)
                mask = jnp.concatenate([mask] * (RAD // 16), axis=0)
                masked[pl.ds(pl.multiple_of(s * 256 + k * RAD, RAD), RAD), :] = unit[:RAD] * mask
            index = (neighbours[pl.ds(s, 1), pl.ds(start, BLK)] - start).astype(F32)
            for tile in range(WIN // 256):
                onehot[
                    block,
                    tile * 256 : (tile + 1) * 256,
                    pl.ds(pl.multiple_of(s * BLK, BLK), BLK),
                ] = one_hot_rows(index, tile, iota_ref[...])
            return 0

        lax.fori_loop(0, FAN, slot, 0, unroll=2)
        summed = dot(w_first[...], masked[...])
        scaled = (summed / math.sqrt(FAN)).astype(BF16)
        half = dot(mix_t[0], scaled) * 0.5
        kinds = jnp.broadcast_to(species[:, pl.ds(start, BLK)], (16, BLK))
        own_hot = (kinds == lax.broadcasted_iota(I32, (16, BLK), 0)).astype(F32).astype(BF16)
        h0 = dot(emb_t[:, :16], own_hot)
        t1[:, pl.ds(pl.multiple_of(start + HALO, BLK), BLK)] = (
            h0 + (half + half * jnp.tanh(half))
        ).astype(BF16)
        return 0

    lax.fori_loop(0, BLOCKS, first_block, 0)

    for tile in range(ATOMS // 256):
        for side in range(2):
            cols = slice(side * HALO, (side + 1) * HALO)
            sendhot[tile * 256 : (tile + 1) * 256, cols] = one_hot_rows(
                send_list[:, cols].astype(F32), tile, iota_ref[...]
            )

    def lend(phase, table):
        sendh[phase] = dot(table[:, HALO : HALO + ATOMS], sendhot[...]).astype(BF16)

    lend(0, t1)
    back_sq, fore_sq = reduce_wait(0, 2)
    back_len = jnp.sqrt(back_sq + 1e-06)
    fore_len = jnp.sqrt(fore_sq + 1e-06)
    here = pos[0]
    tangent = (here - band[0]) / back_len + (band[1] - here) / fore_len
    for copy in h_copies(0, t1):
        copy.start()
    reduce_start(1, (total(tangent * tangent),))

    def second_block(i, _):
        block = order(i)
        start = pl.multiple_of(block * BLK, BLK)

        @pl.when(i == 2)
        def _():
            for copy in h_copies(0, t1):
                copy.wait()

        def slot(s, acc):
            near = t1[:, pl.ds(start, WIN)]
            far = dot(near, onehot[block, :, pl.ds(pl.multiple_of(s * BLK, BLK), BLK)])
            field = dot(rad_t[1], hid[0, pl.ds(pl.multiple_of(s * RAD, RAD), RAD), pl.ds(start, BLK)])
            return acc + far * field

        summed = lax.fori_loop(0, FAN, slot, jnp.zeros((C, BLK), F32), unroll=2)
        scaled = (summed / math.sqrt(FAN)).astype(BF16)
        half = dot(mix_t[1], scaled) * 0.5
        own = pl.ds(pl.multiple_of(start + HALO, BLK), BLK)
        t2[:, own] = (t1[:, own].astype(F32) + (half + half * jnp.tanh(half))).astype(BF16)
        return 0

    lax.fori_loop(0, BLOCKS, second_block, 0)
    lend(1, t2)
    (tau_sq,) = reduce_wait(1, 1)
    for copy in h_copies(1, t2):
        copy.start()

    def force_block(i, _):
        block = order(i)
        start = pl.multiple_of(block * BLK, BLK)

        @pl.when(i == 2)
        def _():
            for copy in h_copies(1, t2):
                copy.wait()

        own = t2[:, pl.ds(pl.multiple_of(start + HALO, BLK), BLK)].astype(F32)

        def slot(s, acc):
            near = t2[:, pl.ds(start, WIN)]
            far = dot(near, onehot[block, :, pl.ds(pl.multiple_of(s * BLK, BLK), BLK)])
            field = dot(rad_t[2], hid[1, pl.ds(pl.multiple_of(s * RAD, RAD), RAD), pl.ds(start, BLK)])
            pair = jnp.sum(field * own * far, axis=0, keepdims=True)
            return tuple(
                acc[comp] + pair * delta[comp, pl.ds(s, 1), pl.ds(start, BLK)] for comp in range(3)
            )

        zero = jnp.zeros((1, BLK), F32)
        parts = lax.fori_loop(0, FAN, slot, (zero, zero, zero), unroll=2)
        for comp in range(3):
            force[comp : comp + 1, pl.ds(start, BLK)] = parts[comp] * (1.0 / math.sqrt(C))
        return 0

    lax.fori_loop(0, BLOCKS, force_block, 0)

    per_atom = dot(jnp.broadcast_to(w_energy[...], (16, C)), t2[:, HALO : HALO + ATOMS])[0:1, :]
    for k in range(SPECIES):
        per_atom = per_atom + jnp.where(species[...] == k, ref_energy[k], 0.0)
    pull = force[0:3, :]
    reduce_start(
        2, (jnp.sum(per_atom, axis=1, keepdims=True), total(pull * tangent))
    )
    energy, along = reduce_wait(2, 2)
    energy_out[...] = energy / (ATOMS * n_atom)
    proj = along / tau_sq
    interior = (
        pull - proj * tangent + SPRING * (fore_len - back_len) / jnp.sqrt(tau_sq) * tangent
    )
    climbing = pull - 2.0 * proj * tangent
    is_end = jnp.logical_or(img == 0, img == n_img - 1)
    band_force = jnp.where(climb[...] == 1, climbing, interior)
    out[0] = jnp.where(is_end, pull, band_force)


def on_device(
    n_img,
    n_atom,
    positions,
    species,
    counts,
    neighbours,
    send_list,
    climb,
    embed,
    ref_energy,
    rad_in,
    rad_out,
    mixing,
    w_energy,
):
    vmem = pl.BlockSpec(memory_space=pltpu.VMEM)
    smem = pl.BlockSpec(memory_space=pltpu.SMEM)
    dma = pltpu.SemaphoreType.DMA
    result, energy = pl.pallas_call(
        functools.partial(kernel, n_img, n_atom),
        out_shape=(
            jax.ShapeDtypeStruct((1, 3, ATOMS), F32),
            jax.ShapeDtypeStruct((1, 1), F32),
        ),
        in_specs=[vmem, vmem, vmem, vmem, vmem, vmem, vmem, smem, vmem, vmem, vmem, vmem],
        out_specs=(vmem, vmem),
        scratch_shapes=[
            pltpu.VMEM((8, TABLE), F32),
            pltpu.VMEM((8, 2 * HALO), F32),
            pltpu.VMEM((2, 3, ATOMS), F32),
            pltpu.VMEM((C, TABLE), BF16),
            pltpu.VMEM((C, TABLE), BF16),
            pltpu.VMEM((2, C, 2 * HALO), BF16),
            pltpu.VMEM((BLOCKS, WIN, FAN * BLK), BF16),
            pltpu.VMEM((ATOMS, 2 * HALO), BF16),
            pltpu.VMEM((256, BLK), BF16),
            pltpu.VMEM((2, FAN * RAD, ATOMS), BF16),
            pltpu.VMEM((FAN * 256, BLK), BF16),
            pltpu.VMEM((FAN * 192, C), BF16),
            pltpu.VMEM((C, FAN * 256), BF16),
            pltpu.VMEM((3, C, RAD), BF16),
            pltpu.VMEM((2, C, C), BF16),
            pltpu.VMEM((C, C), BF16),
            pltpu.VMEM((C, BLK), BF16),
            pltpu.VMEM((SPECIES, FAN, BLK), F32),
            pltpu.VMEM((FAN, BLK), F32),
            pltpu.VMEM((3, FAN, ATOMS), F32),
            pltpu.VMEM((8, ATOMS), F32),
            pltpu.VMEM((3, n_atom, 1, LANES), F32),
            dma((2,)),
            dma((2,)),
            dma((2,)),
            dma((2,)),
            dma((2, 2)),
            dma((2, 2)),
            dma((3, n_atom)),
            dma((3, n_atom)),
        ],
        compiler_params=pltpu.CompilerParams(
            collective_id=0, has_side_effects=True, vmem_limit_bytes=60 * 1024 * 1024
        ),
        name="band_step",
    )(
        positions,
        species.reshape(1, ATOMS),
        counts.reshape(1, ATOMS),
        neighbours,
        send_list.reshape(1, 2 * HALO),
        climb.reshape(1, 1),
        embed,
        ref_energy,
        rad_in,
        rad_out,
        mixing,
        w_energy.reshape(1, C),
    )
    return result, energy.reshape(1)


def solution(mesh):
    return jax.shard_map(
        functools.partial(on_device, mesh.shape["img"], mesh.shape["atom"]),
        mesh=mesh,
        in_specs=(
            P("img", None, "atom"),
            P("atom"),
            P("atom"),
            P(None, "atom"),
            P("atom"),
            P("img"),
            P(),
            P(),
            P(),
            P(),
            P(),
            P(),
        ),
        out_specs=(P("img", None, "atom"), P("img")),
        check_vma=False,
    )
```

time: 344 us -> 61.8 us (0.18)
  the two profiles are of different devices: /device:TPU:6 before, /device:TPU:1 now
where the time goes in v1:
time: 61.8 us; the launch traced here: 61.5 us
  Pallas kernels  55.8 us (90%)
  between operations  3.05 us (5%)
  local copies, waits for them, and re-layouts  2.64 us (4%)
    pallas_call x1, Pallas kernels, on_device(): pl.pallas_call(functools.partial(kernel, n_img, n_atom), out_shape=(jax.S...  55.8 us
    unnamed x2, local copies, waits for them, and re-layouts  2.64 us

profile of v1, /device:TPU:1, one launch (start us, length us, event | category | flops | bytes accessed | tf_op | source)
XLA Modules:
  0.0 61.5 jit_solution(7888678719871523675)
XLA Ops:
  1.3 1.3 %copy.14.pos = f32[1,3,1024]{2,1,0:T(4,128)} copy(f32[1,3,1024]{2,0,1:T(1,128)} %param.12) | data formatting | bytes 24576 | tf_op args[0]
  2.6 55.8 %band_step.1 = (f32[1,3,1024]{2,1,0:T(4,128)}, f32[1,1]{1,0:T(1,128)}) custom-call(f32[1,3,1024]{2,1,0:T(4,128)} %copy.14.pos, s32[1,1024]{1,0:T(1,128)} %bitcast.7, s32[1,1024]{1,0:T(1,128)} %bitcast.8, s32[16,1024]{1,0:T(8,128)} %neighbours.1, s32[1,512]{1,0:T(1,128)} %bitcast.9, s32[1,1]{1,0:T(1,128)} %bitcast.6.climb, bf16[4,128]{1,0:T(4,128)(2,1)} %embed.1, ...), custom_call_target="tpu_custom_call" | custom-call | tf_op jit(solution)/shard_map/band_step/pallas_call | solution.py:457
  58.4 1.3 %copy.15 = f32[1,3,1024]{2,0,1:T(1,128)} copy(f32[1,3,1024]{2,1,0:T(4,128)} %get-tuple-element.6) | data formatting | bytes 24576

commit v2 on v1

v2 whole, which is shorter than its diff:
```python
import functools
import math

import jax
import jax.numpy as jnp
from jax import lax
from jax.experimental import pallas as pl
from jax.experimental.pallas import tpu as pltpu
from jax.sharding import PartitionSpec as P

F32 = jnp.float32
BF16 = jnp.bfloat16
I32 = jnp.int32
MESH = pl.DeviceIdType.MESH

SPRING = 5.0
C = 128
RAD = 64
NB = 8
SPECIES = 4
FAN = 16
HALO = 256
ATOMS = 1024
BLK = 256
BLOCKS = ATOMS // BLK
LANES = 128
WIN = LANES + 2 * HALO
TILES = ATOMS // LANES
TABLE = ATOMS + 2 * HALO
UNROLL = 4
FAR_AWAY = 1.0e4


def lane_gather(source, index):
    return jnp.take_along_axis(source, index, axis=1, mode="promise_in_bounds")


def dot(a, b):
    return jnp.dot(a, b, preferred_element_type=F32)


def total(x):
    return jnp.sum(jnp.sum(x, axis=0, keepdims=True), axis=1, keepdims=True)


def one_hot_rows(local, iota):
    local = jnp.broadcast_to(local, (16, LANES)).astype(BF16)
    local = jnp.concatenate([local] * 16, axis=0)
    return jnp.where(local == iota, jnp.ones_like(iota), jnp.zeros_like(iota))


def side_by_side(left, right):
    return jnp.concatenate([left, right], axis=1)


def tile_of(lane):
    return slice(lane * LANES, (lane + 1) * LANES)


def kernel(
    n_img,
    n_atom,
    pos,
    species,
    counts,
    neighbours,
    send_list,
    climb,
    embed,
    ref_energy,
    rad_in,
    rad_out,
    mixing,
    w_energy,
    out,
    energy_out,
    ptab,
    sendpos,
    band,
    t1,
    t2,
    sendh,
    onehot,
    sendhot,
    iota_ref,
    hid,
    masked,
    w_hid,
    w_first,
    rad_t,
    mix_t,
    emb_t,
    basis,
    sp_mask,
    delta,
    rel,
    scaled_ref,
    last_ref,
    own_ref,
    force,
    tang,
    rbuf,
    pos_send,
    pos_recv,
    img_send,
    img_recv,
    h_send,
    h_recv,
    r_send,
    r_recv,
):
    img = lax.axis_index("img")
    me = lax.axis_index("atom")

    def ring(index, step, size):
        moved = index + step
        return jnp.where(moved >= size, moved - size, moved)

    up = ring(me, 1, n_atom)
    down = ring(me, n_atom - 1, n_atom)
    img_up = ring(img, 1, n_img)
    img_down = ring(img, n_img - 1, n_img)

    barrier = pltpu.get_barrier_semaphore()
    for d in range(1, n_atom):
        pl.semaphore_signal(
            barrier, inc=1, device_id=(img, ring(me, d, n_atom)), device_id_type=MESH
        )
    for other in (img_up, img_down):
        pl.semaphore_signal(barrier, inc=1, device_id=(other, me), device_id_type=MESH)

    own_cols = slice(HALO, HALO + ATOMS)
    for comp in range(3):
        ptab[comp : comp + 1, own_cols] = pos[comp]
    ptab[3:4, own_cols] = species[...].astype(F32)
    ptab[4:8, own_cols] = jnp.zeros((4, ATOMS), F32)
    for t in range(4):
        index = jnp.broadcast_to(send_list[:, tile_of(t)], (8, LANES))
        low = index & 127
        high = index >> 7
        got = jnp.zeros((8, LANES), F32)
        for w in range(ATOMS // LANES):
            source = ptab[:, HALO + w * LANES : HALO + (w + 1) * LANES]
            got = jnp.where(high == w, lane_gather(source, low), got)
        sendpos[:, tile_of(t)] = got

    iota_ref[...] = lax.broadcasted_iota(I32, (256, LANES), 0).astype(F32).astype(BF16)
    for layer in range(3):
        rad_t[layer] = rad_out[layer].astype(F32).T.astype(BF16)
    for layer in range(2):
        mix_t[layer] = mixing[layer].astype(F32).T.astype(BF16)
    emb = embed[...].astype(F32)
    emb_rows = jnp.concatenate([emb, jnp.zeros((C - SPECIES, C), F32)], axis=0)
    emb_t[...] = emb_rows.T.astype(BF16)
    first = rad_out[0].astype(F32)
    w0 = jnp.concatenate([first * emb[k : k + 1, :] for k in range(SPECIES)], axis=0).T.astype(BF16)
    for s in range(FAN):
        w_first[:, s * 256 : (s + 1) * 256] = w0
    lane = lax.broadcasted_iota(I32, (NB, C), 1)
    spread = (lane // FAN == lax.broadcasted_iota(I32, (NB, C), 0)).astype(F32).astype(BF16)
    lane64 = lax.broadcasted_iota(I32, (RAD, C), 1) % FAN
    for layer in range(3):
        wide = lax.dot_general(
            rad_in[layer], spread, (((0,), (0,)), ((), ())), preferred_element_type=F32
        )
        wide = wide * 0.5
        for s in range(FAN):
            start = s * 192 + layer * RAD
            w_hid[start : start + RAD, :] = jnp.where(lane64 == s, wide, 0.0).astype(BF16)

    def copy_to(source, target, send, recv, device):
        return pltpu.make_async_remote_copy(
            src_ref=source,
            dst_ref=target,
            send_sem=send,
            recv_sem=recv,
            device_id=device,
            device_id_type=MESH,
        )

    def pos_copies():
        low, high = slice(0, HALO), slice(HALO + ATOMS, TABLE)
        return (
            copy_to(
                sendpos.at[:, 0:HALO], ptab.at[:, high], pos_send.at[0], pos_recv.at[0], (img, down)
            ),
            copy_to(
                sendpos.at[:, HALO : 2 * HALO],
                ptab.at[:, low],
                pos_send.at[1],
                pos_recv.at[1],
                (img, up),
            ),
        )

    def img_copies():
        return (
            copy_to(pos, band.at[0], img_send.at[0], img_recv.at[0], (img_up, me)),
            copy_to(pos, band.at[1], img_send.at[1], img_recv.at[1], (img_down, me)),
        )

    def h_copies(phase, table):
        return (
            copy_to(
                sendh.at[phase, 0:2],
                table.at[10:12],
                h_send.at[phase, 0],
                h_recv.at[phase, 0],
                (img, down),
            ),
            copy_to(
                sendh.at[phase, 2:4],
                table.at[0:2],
                h_send.at[phase, 1],
                h_recv.at[phase, 1],
                (img, up),
            ),
        )

    lane_row = lax.broadcasted_iota(I32, (1, LANES), 1)

    def reduce_start(phase, values):
        message = jnp.zeros((1, LANES), F32)
        for n, value in enumerate(values):
            message = jnp.where(lane_row == n, value, message)
        rbuf[phase, me] = message
        for d in range(1, n_atom):
            copy_to(
                rbuf.at[phase, me],
                rbuf.at[phase, me],
                r_send.at[phase],
                r_recv.at[phase],
                (img, ring(me, d, n_atom)),
            ).start()

    def reduce_wait(phase, number):
        others = rbuf.at[phase, 0 : n_atom - 1]
        arrived = copy_to(others, others, r_send.at[phase], r_recv.at[phase], (img, up))
        arrived.wait_send()
        arrived.wait_recv()
        summed = jnp.sum(rbuf[phase], axis=0)
        return [
            jnp.sum(jnp.where(lane_row == n, summed, 0.0), axis=1, keepdims=True)
            for n in range(number)
        ]

    def first_block(i, _):
        block = lax.rem(i + 1, BLOCKS)
        start = pl.multiple_of(block * BLK, BLK)

        @pl.when(i == 1)
        def _():
            pl.semaphore_wait(barrier, n_atom + 1)
            for copy in pos_copies() + img_copies():
                copy.start()

        @pl.when(i == 2)
        def _():
            for copy in pos_copies() + img_copies():
                copy.wait()
            behind = pos[...] - band[0]
            ahead = band[1] - pos[...]
            reduce_start(
                0, (total(jnp.sum(behind * behind, axis=0)), total(jnp.sum(ahead * ahead, axis=0)))
            )

        for t in range(BLK // LANES):
            at = pl.multiple_of(start + t * LANES, LANES)
            tile = block * 2 + t
            offset = neighbours[:, pl.ds(at, LANES)] - at
            rel[tile] = offset
            low = offset & 127
            high = offset >> 7
            got = [None] * 4
            for w in range(WIN // LANES):
                here = high == w
                for comp in range(4):
                    source = jnp.broadcast_to(
                        ptab[comp : comp + 1, pl.ds(pl.multiple_of(at + w * LANES, LANES), LANES)],
                        (FAN, LANES),
                    )
                    value = lane_gather(source, low)
                    got[comp] = value if w == 0 else jnp.where(here, value, got[comp])
            slots = lax.broadcasted_iota(I32, (FAN, LANES), 0)
            live = slots < counts[:, pl.ds(at, LANES)]
            dist = jnp.zeros((FAN, LANES), F32)
            for comp in range(3):
                diff = got[comp] - pos[comp, :, pl.ds(at, LANES)]
                delta[comp, tile] = diff
                dist = dist + diff * diff
            dist = jnp.where(live, dist, FAR_AWAY)
            for k in range(NB):
                shifted = dist - 2.0 * k
                basis[t, k * FAN : (k + 1) * FAN, :] = jnp.exp(-(shifted * shifted) / 8.0).astype(
                    BF16
                )
            for k in range(SPECIES):
                sp_mask[t, k] = (got[3] == float(k)).astype(F32)

        def slot(s, _):
            rows = pl.multiple_of(s * 192, 192)
            half = dot(w_hid[pl.ds(rows, 192), :], side_by_side(basis[0], basis[1]))
            unit = (half + half * jnp.tanh(half)).astype(BF16)
            at_row = pl.multiple_of(s * RAD, RAD)
            for t in range(BLK // LANES):
                tile = block * 2 + t
                for layer in (1, 2):
                    hid[layer - 1, tile, pl.ds(at_row, RAD), :] = unit[
                        layer * RAD : (layer + 1) * RAD, tile_of(t)
                    ]
                for k in range(SPECIES):
                    mask = jnp.broadcast_to(sp_mask[t, k, pl.ds(s, 1), :], (16, LANES)).astype(BF16)
                    mask = jnp.concatenate([mask] * (RAD // 16), axis=0)
                    masked[t, pl.ds(pl.multiple_of(s * 256 + k * RAD, RAD), RAD), :] = (
                        unit[:RAD, tile_of(t)] * mask
                    )
                index = rel[tile, pl.ds(s, 1), :] & 255
                onehot[tile, s] = one_hot_rows(index.astype(F32), iota_ref[...])
            return 0

        lax.fori_loop(0, FAN, slot, 0, unroll=2)
        summed = dot(w_first[...], side_by_side(masked[0], masked[1]))
        scaled = (summed / math.sqrt(FAN)).astype(BF16)
        half = dot(mix_t[0], scaled) * 0.5
        kinds = jnp.broadcast_to(species[:, pl.ds(start, BLK)], (16, BLK))
        own_hot = (kinds == lax.broadcasted_iota(I32, (16, BLK), 0)).astype(F32).astype(BF16)
        h1 = (dot(emb_t[:, :16], own_hot) + (half + half * jnp.tanh(half))).astype(BF16)
        for t in range(BLK // LANES):
            t1[block * 2 + t + 2] = h1[:, tile_of(t)]
        return 0

    lax.fori_loop(0, BLOCKS, first_block, 0)

    for t in range(2 * HALO // LANES):
        index = send_list[:, tile_of(t)].astype(F32)
        for part in range(ATOMS // 256):
            local = index - 256.0 * part
            inside = jnp.logical_and(local >= 0.0, local < 256.0)
            sendhot[t, part * 256 : (part + 1) * 256, :] = one_hot_rows(
                jnp.where(inside, local, -1.0), iota_ref[...]
            )

    def lend(phase, table):
        own = jnp.concatenate([table[2 + t] for t in range(8)], axis=1)
        for side in range(2):
            lent = dot(own, side_by_side(sendhot[2 * side], sendhot[2 * side + 1])).astype(BF16)
            for t in range(2):
                sendh[phase, 2 * side + t] = lent[:, tile_of(t)]

    lend(0, t1)
    back_sq, fore_sq = reduce_wait(0, 2)
    back_len = jnp.sqrt(back_sq + 1e-06)
    fore_len = jnp.sqrt(fore_sq + 1e-06)
    tangent = (pos[...] - band[0]) / back_len + (band[1] - pos[...]) / fore_len
    tang[...] = tangent
    for copy in h_copies(0, t1):
        copy.start()
    reduce_start(1, (total(jnp.sum(tangent * tangent, axis=0)),))

    def gathered(table, layer, tile, pair):
        s = 2 * pair
        hot = side_by_side(onehot[tile, s], onehot[tile, s + 1])
        fars = [
            dot(side_by_side(table[tile + 2 * part], table[tile + 2 * part + 1]), hot)
            for part in range(2)
        ]
        rows = pl.multiple_of(s * RAD, 2 * RAD)
        both = hid[layer, tile, pl.ds(rows, 2 * RAD), :]
        field = dot(rad_t[layer + 1], side_by_side(both[:RAD], both[RAD:]))
        far = []
        for side in range(2):
            index = jnp.broadcast_to(rel[tile, pl.ds(s + side, 1), :], (8, LANES))
            low = index & 127
            second = (index >> 8) == 1
            third = (index >> 8) == 2
            pieces = []
            for g in range(C // 8):
                rows8 = slice(8 * g, 8 * g + 8)
                value = jnp.where(second, fars[1][rows8, tile_of(side)], fars[0][rows8, tile_of(side)])
                pieces.append(jnp.where(third, lane_gather(last_ref[rows8, :], low), value))
            far.append(jnp.concatenate(pieces, axis=0))
        return far, field

    def tile_loop(table, phase, body):
        def step(i, _):
            tile = lax.rem(i + 2, TILES)

            @pl.when(i == 4)
            def _():
                for copy in h_copies(phase, table):
                    copy.wait()

            last_ref[...] = table[tile + 4].astype(F32)
            body(tile)
            return 0

        lax.fori_loop(0, TILES, step, 0)

    def second_tile(tile):
        def pair(p, acc):
            far, field = gathered(t1, 0, tile, p)
            return acc + (far[0] * field[:, tile_of(0)] + far[1] * field[:, tile_of(1)])

        summed = lax.fori_loop(0, FAN // 2, pair, jnp.zeros((C, LANES), F32), unroll=UNROLL)
        scaled_ref[tile] = (summed / math.sqrt(FAN)).astype(BF16)

    tile_loop(t1, 0, second_tile)
    for t in range(0, TILES, 2):
        half = dot(mix_t[1], side_by_side(scaled_ref[t], scaled_ref[t + 1])) * 0.5
        update = half + half * jnp.tanh(half)
        for side in range(2):
            at = t + side + 2
            t2[at] = (t1[at].astype(F32) + update[:, tile_of(side)]).astype(BF16)
    lend(1, t2)
    (tau_sq,) = reduce_wait(1, 1)
    for copy in h_copies(1, t2):
        copy.start()

    def force_tile(tile):
        at = pl.multiple_of(tile * LANES, LANES)
        own_ref[...] = t2[tile + 2].astype(F32)

        def pair(p, acc):
            far, field = gathered(t2, 1, tile, p)
            for side in range(2):
                work = far[side] * field[:, tile_of(side)] * own_ref[...]
                strip = jnp.sum(work.reshape(C // 8, 8, LANES), axis=0)
                acc = tuple(
                    acc[comp] + strip * delta[comp, tile, pl.ds(2 * p + side, 1), :]
                    for comp in range(3)
                )
            return acc

        zero = jnp.zeros((8, LANES), F32)
        parts = lax.fori_loop(0, FAN // 2, pair, (zero, zero, zero), unroll=UNROLL)
        for comp in range(3):
            force[comp, :, pl.ds(at, LANES)] = jnp.sum(parts[comp], axis=0, keepdims=True) * (
                1.0 / math.sqrt(C)
            )

    tile_loop(t2, 1, force_tile)

    own = jnp.concatenate([t2[2 + t] for t in range(8)], axis=1)
    per_atom = dot(jnp.broadcast_to(w_energy[...], (16, C)), own)[0:1, :]
    for k in range(SPECIES):
        per_atom = per_atom + jnp.where(species[...] == k, ref_energy[k], 0.0)
    pull = force[...]
    tangent = tang[...]
    reduce_start(
        2,
        (
            jnp.sum(per_atom, axis=1, keepdims=True),
            total(jnp.sum(pull * tangent, axis=0)),
        ),
    )
    energy, along = reduce_wait(2, 2)
    energy_out[...] = energy / (ATOMS * n_atom)
    proj = along / tau_sq
    interior = (
        pull - proj * tangent + SPRING * (fore_len - back_len) / jnp.sqrt(tau_sq) * tangent
    )
    climbing = pull - 2.0 * proj * tangent
    is_end = jnp.logical_or(img == 0, img == n_img - 1)
    band_force = jnp.where(climb[...] == 1, climbing, interior)
    out[...] = jnp.where(is_end, pull, band_force)


def on_device(
    n_img,
    n_atom,
    positions,
    species,
    counts,
    neighbours,
    send_list,
    climb,
    embed,
    ref_energy,
    rad_in,
    rad_out,
    mixing,
    w_energy,
):
    vmem = pl.BlockSpec(memory_space=pltpu.VMEM)
    smem = pl.BlockSpec(memory_space=pltpu.SMEM)
    dma = pltpu.SemaphoreType.DMA
    result, energy = pl.pallas_call(
        functools.partial(kernel, n_img, n_atom),
        out_shape=(
            jax.ShapeDtypeStruct((3, 1, ATOMS), F32),
            jax.ShapeDtypeStruct((1, 1), F32),
        ),
        in_specs=[vmem, vmem, vmem, vmem, vmem, vmem, vmem, smem, vmem, vmem, vmem, vmem],
        out_specs=(vmem, vmem),
        scratch_shapes=[
            pltpu.VMEM((8, TABLE), F32),
            pltpu.VMEM((8, 2 * HALO), F32),
            pltpu.VMEM((2, 3, 1, ATOMS), F32),
            pltpu.VMEM((12, C, LANES), BF16),
            pltpu.VMEM((12, C, LANES), BF16),
            pltpu.VMEM((2, 4, C, LANES), BF16),
            pltpu.VMEM((TILES, FAN, 256, LANES), BF16),
            pltpu.VMEM((4, ATOMS, LANES), BF16),
            pltpu.VMEM((256, LANES), BF16),
            pltpu.VMEM((2, TILES, FAN * RAD, LANES), BF16),
            pltpu.VMEM((2, FAN * 256, LANES), BF16),
            pltpu.VMEM((FAN * 192, C), BF16),
            pltpu.VMEM((C, FAN * 256), BF16),
            pltpu.VMEM((3, C, RAD), BF16),
            pltpu.VMEM((2, C, C), BF16),
            pltpu.VMEM((C, C), BF16),
            pltpu.VMEM((2, C, LANES), BF16),
            pltpu.VMEM((2, SPECIES, FAN, LANES), F32),
            pltpu.VMEM((3, TILES, FAN, LANES), F32),
            pltpu.VMEM((TILES, FAN, LANES), I32),
            pltpu.VMEM((TILES, C, LANES), BF16),
            pltpu.VMEM((C, LANES), F32),
            pltpu.VMEM((C, LANES), F32),
            pltpu.VMEM((3, 1, ATOMS), F32),
            pltpu.VMEM((3, 1, ATOMS), F32),
            pltpu.VMEM((3, n_atom, 1, LANES), F32),
            dma((2,)),
            dma((2,)),
            dma((2,)),
            dma((2,)),
            dma((2, 2)),
            dma((2, 2)),
            dma((3,)),
            dma((3,)),
        ],
        compiler_params=pltpu.CompilerParams(
            collective_id=0, has_side_effects=True, vmem_limit_bytes=60 * 1024 * 1024
        ),
        name="band_step",
    )(
        positions.transpose(1, 0, 2),
        species.reshape(1, ATOMS),
        counts.reshape(1, ATOMS),
        neighbours,
        send_list.reshape(1, 2 * HALO),
        climb.reshape(1, 1),
        embed,
        ref_energy,
        rad_in,
        rad_out,
        mixing,
        w_energy.reshape(1, C),
    )
    return result.transpose(1, 0, 2), energy.reshape(1)


def solution(mesh):
    return jax.shard_map(
        functools.partial(on_device, mesh.shape["img"], mesh.shape["atom"]),
        mesh=mesh,
        in_specs=(
            P("img", None, "atom"),
            P("atom"),
            P("atom"),
            P(None, "atom"),
            P("atom"),
            P("img"),
            P(),
            P(),
            P(),
            P(),
            P(),
            P(),
        ),
        out_specs=(P("img", None, "atom"), P("img")),
        check_vma=False,
    )
```

time: 61.8 us -> 48.9 us (0.79)
  Pallas kernels: 55.8 us -> 44.3 us
  local copies, waits for them, and re-layouts: 2.64 us -> 1.31 us
    pallas_call x1, Pallas kernels: 55.8 us -> 44.3 us  [on_device(): pl.pallas_call(functools.partial(kernel, n_img, n_atom), out_shape=(jax.S...]
    unnamed x2 -> x1, local copies, waits for them, and re-layouts: 2.64 us -> 1.31 us
where the time goes in v2:
time: 48.9 us; the launch traced here: 48.7 us
  Pallas kernels  44.3 us (91%)
  between operations  3.05 us (6%)
  local copies, waits for them, and re-layouts  1.31 us (3%)
    pallas_call x1, Pallas kernels, on_device(): pl.pallas_call(functools.partial(kernel, n_img, n_atom), out_shape=(jax.S...  44.3 us
    unnamed x1, local copies, waits for them, and re-layouts  1.31 us

profile of v2, /device:TPU:1, one launch (start us, length us, event | category | flops | bytes accessed | tf_op | source)
XLA Modules:
  0.0 48.7 jit_solution(11776197168385202968)
XLA Ops:
  1.3 44.3 %band_step.1 = (f32[3,1,1024]{2,1,0:T(1,128)}, f32[1,1]{1,0:T(1,128)}) custom-call(f32[3,1,1024]{2,1,0:T(1,128)} %bitcast.9, s32[1,1024]{1,0:T(1,128)} %bitcast.11, s32[1,1024]{1,0:T(1,128)} %bitcast.12, s32[16,1024]{1,0:T(8,128)} %neighbours.1, s32[1,512]{1,0:T(1,128)} %bitcast.13, s32[1,1]{1,0:T(1,128)} %bitcast.8.climb, bf16[4,128]{1,0:T(4,128)(2,1)} %embed.1, ...), custom_call_target="tpu_custom_call" | custom-call | tf_op jit(solution)/shard_map/band_step/pallas_call | solution.py:487
  45.6 1.3 %copy.17 = f32[1,3,1024]{2,0,1:T(1,128)} copy(f32[1,3,1024]{2,0,1:T(1,128)} %bitcast.10) | data formatting | bytes 24576

commit v3 on v2

--- a/solution.py
+++ b/solution.py
@@ -27,7 +27,8 @@
 WIN = LANES + 2 * HALO
 TILES = ATOMS // LANES
 TABLE = ATOMS + 2 * HALO
-UNROLL = 4
+UNROLL = 8
+HID_UNROLL = 4
 FAR_AWAY = 1.0e4
 
 
@@ -80,18 +81,15 @@
     t1,
     t2,
     sendh,
-    onehot,
     sendhot,
     iota_ref,
     hid,
-    masked,
     w_hid,
-    w_first,
     rad_t,
     mix_t,
     emb_t,
     basis,
-    sp_mask,
+    kind,
     delta,
     rel,
     scaled_ref,
@@ -152,10 +150,6 @@
     emb = embed[...].astype(F32)
     emb_rows = jnp.concatenate([emb, jnp.zeros((C - SPECIES, C), F32)], axis=0)
     emb_t[...] = emb_rows.T.astype(BF16)
-    first = rad_out[0].astype(F32)
-    w0 = jnp.concatenate([first * emb[k : k + 1, :] for k in range(SPECIES)], axis=0).T.astype(BF16)
-    for s in range(FAN):
-        w_first[:, s * 256 : (s + 1) * 256] = w0
     lane = lax.broadcasted_iota(I32, (NB, C), 1)
     spread = (lane // FAN == lax.broadcasted_iota(I32, (NB, C), 0)).astype(F32).astype(BF16)
     lane64 = lax.broadcasted_iota(I32, (RAD, C), 1) % FAN
@@ -294,42 +288,54 @@
                 basis[t, k * FAN : (k + 1) * FAN, :] = jnp.exp(-(shifted * shifted) / 8.0).astype(
                     BF16
                 )
-            for k in range(SPECIES):
-                sp_mask[t, k] = (got[3] == float(k)).astype(F32)
+            kind[tile] = got[3].astype(I32)
 
         def slot(s, _):
             rows = pl.multiple_of(s * 192, 192)
             half = dot(w_hid[pl.ds(rows, 192), :], side_by_side(basis[0], basis[1]))
             unit = (half + half * jnp.tanh(half)).astype(BF16)
-            at_row = pl.multiple_of(s * RAD, RAD)
             for t in range(BLK // LANES):
-                tile = block * 2 + t
-                for layer in (1, 2):
-                    hid[layer - 1, tile, pl.ds(at_row, RAD), :] = unit[
-                        layer * RAD : (layer + 1) * RAD, tile_of(t)
-                    ]
-                for k in range(SPECIES):
-                    mask = jnp.broadcast_to(sp_mask[t, k, pl.ds(s, 1), :], (16, LANES)).astype(BF16)
-                    mask = jnp.concatenate([mask] * (RAD // 16), axis=0)
-                    masked[t, pl.ds(pl.multiple_of(s * 256 + k * RAD, RAD), RAD), :] = (
-                        unit[:RAD, tile_of(t)] * mask
-                    )
-                index = rel[tile, pl.ds(s, 1), :] & 255
-                onehot[tile, s] = one_hot_rows(index.astype(F32), iota_ref[...])
+                hid[block * 2 + t, pl.ds(rows, 192), :] = unit[:, tile_of(t)]
             return 0
 
-        lax.fori_loop(0, FAN, slot, 0, unroll=2)
-        summed = dot(w_first[...], side_by_side(masked[0], masked[1]))
-        scaled = (summed / math.sqrt(FAN)).astype(BF16)
-        half = dot(mix_t[0], scaled) * 0.5
-        kinds = jnp.broadcast_to(species[:, pl.ds(start, BLK)], (16, BLK))
-        own_hot = (kinds == lax.broadcasted_iota(I32, (16, BLK), 0)).astype(F32).astype(BF16)
-        h1 = (dot(emb_t[:, :16], own_hot) + (half + half * jnp.tanh(half))).astype(BF16)
-        for t in range(BLK // LANES):
-            t1[block * 2 + t + 2] = h1[:, tile_of(t)]
+        lax.fori_loop(0, FAN, slot, 0, unroll=HID_UNROLL)
         return 0
 
     lax.fori_loop(0, BLOCKS, first_block, 0)
+
+    def radial(layer, tile, pair):
+        sides = [
+            hid[tile, pl.ds(pl.multiple_of((2 * pair + n) * 192 + layer * RAD, RAD), RAD), :]
+            for n in range(2)
+        ]
+        return dot(rad_t[layer], side_by_side(*sides))
+
+    def update_of(layer, t):
+        half = dot(mix_t[layer], side_by_side(scaled_ref[t], scaled_ref[t + 1])) * 0.5
+        return half + half * jnp.tanh(half)
+
+    last_ref[...] = emb_t[...].astype(F32)
+
+    def first_tile(tile, _):
+        def pair(p, acc):
+            field = radial(0, tile, p)
+            for side in range(2):
+                index = jnp.broadcast_to(kind[tile, pl.ds(2 * p + side, 1), :], (8, LANES))
+                far = [lane_gather(last_ref[8 * g : 8 * g + 8, :], index) for g in range(C // 8)]
+                acc = acc + jnp.concatenate(far, axis=0) * field[:, tile_of(side)]
+            return acc
+
+        summed = lax.fori_loop(0, FAN // 2, pair, jnp.zeros((C, LANES), F32), unroll=UNROLL)
+        scaled_ref[tile] = (summed / math.sqrt(FAN)).astype(BF16)
+        return 0
+
+    lax.fori_loop(0, TILES, first_tile, 0)
+    for t in range(0, TILES, 2):
+        kinds = jnp.broadcast_to(species[:, t * LANES : (t + 2) * LANES], (16, 2 * LANES))
+        own_hot = (kinds == lax.broadcasted_iota(I32, kinds.shape, 0)).astype(F32).astype(BF16)
+        h1 = (dot(emb_t[:, :16], own_hot) + update_of(0, t)).astype(BF16)
+        for side in range(2):
+            t1[t + side + 2] = h1[:, tile_of(side)]
 
     for t in range(2 * HALO // LANES):
         index = send_list[:, tile_of(t)].astype(F32)
@@ -358,18 +364,21 @@
     reduce_start(1, (total(jnp.sum(tangent * tangent, axis=0)),))
 
     def gathered(table, layer, tile, pair):
-        s = 2 * pair
-        hot = side_by_side(onehot[tile, s], onehot[tile, s + 1])
-        fars = [
-            dot(side_by_side(table[tile + 2 * part], table[tile + 2 * part + 1]), hot)
-            for part in range(2)
-        ]
-        rows = pl.multiple_of(s * RAD, 2 * RAD)
-        both = hid[layer, tile, pl.ds(rows, 2 * RAD), :]
-        field = dot(rad_t[layer + 1], side_by_side(both[:RAD], both[RAD:]))
+        hot = side_by_side(
+            *[
+                one_hot_rows((rel[tile, pl.ds(2 * pair + n, 1), :] & 255).astype(F32), iota_ref[...])
+                for n in range(2)
+            ]
+        )
+        near = jnp.concatenate(
+            [side_by_side(table[tile + 2 * n], table[tile + 2 * n + 1]) for n in range(2)], axis=0
+        )
+        both = dot(near, hot)
+        fars = both[:C], both[C:]
+        field = radial(layer + 1, tile, pair)
         far = []
         for side in range(2):
-            index = jnp.broadcast_to(rel[tile, pl.ds(s + side, 1), :], (8, LANES))
+            index = jnp.broadcast_to(rel[tile, pl.ds(2 * pair + side, 1), :], (8, LANES))
             low = index & 127
             second = (index >> 8) == 1
             third = (index >> 8) == 2
@@ -406,8 +415,7 @@
 
     tile_loop(t1, 0, second_tile)
     for t in range(0, TILES, 2):
-        half = dot(mix_t[1], side_by_side(scaled_ref[t], scaled_ref[t + 1])) * 0.5
-        update = half + half * jnp.tanh(half)
+        update = update_of(1, t)
         for side in range(2):
             at = t + side + 2
             t2[at] = (t1[at].astype(F32) + update[:, tile_of(side)]).astype(BF16)
@@ -499,18 +507,15 @@
             pltpu.VMEM((12, C, LANES), BF16),
             pltpu.VMEM((12, C, LANES), BF16),
             pltpu.VMEM((2, 4, C, LANES), BF16),
-            pltpu.VMEM((TILES, FAN, 256, LANES), BF16),
             pltpu.VMEM((4, ATOMS, LANES), BF16),
             pltpu.VMEM((256, LANES), BF16),
-            pltpu.VMEM((2, TILES, FAN * RAD, LANES), BF16),
-            pltpu.VMEM((2, FAN * 256, LANES), BF16),
+            pltpu.VMEM((TILES, FAN * 192, LANES), BF16),
             pltpu.VMEM((FAN * 192, C), BF16),
-            pltpu.VMEM((C, FAN * 256), BF16),
             pltpu.VMEM((3, C, RAD), BF16),
             pltpu.VMEM((2, C, C), BF16),
             pltpu.VMEM((C, C), BF16),
             pltpu.VMEM((2, C, LANES), BF16),
-            pltpu.VMEM((2, SPECIES, FAN, LANES), F32),
+            pltpu.VMEM((TILES, FAN, LANES), I32),
             pltpu.VMEM((3, TILES, FAN, LANES), F32),
             pltpu.VMEM((TILES, FAN, LANES), I32),
             pltpu.VMEM((TILES, C, LANES), BF16),

time: 48.9 us -> 47.4 us (0.969)
  Pallas kernels: 44.3 us -> 42.8 us
    pallas_call x1, Pallas kernels: 44.3 us -> 42.8 us  [on_device(): pl.pallas_call(functools.partial(kernel, n_img, n_atom), out_shape=(jax.S...]
where the time goes in v3:
time: 47.4 us; the launch traced here: 47.2 us
  Pallas kernels  42.8 us (90%)
  between operations  3.05 us (6%)
  local copies, waits for them, and re-layouts  1.31 us (3%)
    pallas_call x1, Pallas kernels, on_device(): pl.pallas_call(functools.partial(kernel, n_img, n_atom), out_shape=(jax.S...  42.8 us
    unnamed x1, local copies, waits for them, and re-layouts  1.31 us

profile of v3, /device:TPU:1, one launch (start us, length us, event | category | flops | bytes accessed | tf_op | source)
XLA Modules:
  0.0 47.2 jit_solution(16718086228842508502)
XLA Ops:
  1.3 42.8 %band_step.1 = (f32[3,1,1024]{2,1,0:T(1,128)}, f32[1,1]{1,0:T(1,128)}) custom-call(f32[3,1,1024]{2,1,0:T(1,128)} %bitcast.9, s32[1,1024]{1,0:T(1,128)} %bitcast.11, s32[1,1024]{1,0:T(1,128)} %bitcast.12, s32[16,1024]{1,0:T(8,128)} %neighbours.1, s32[1,512]{1,0:T(1,128)} %bitcast.13, s32[1,1]{1,0:T(1,128)} %bitcast.8.climb, bf16[4,128]{1,0:T(4,128)(2,1)} %embed.1, ...), custom_call_target="tpu_custom_call" | custom-call | tf_op jit(solution)/shard_map/band_step/pallas_call | solution.py:495
  44.1 1.3 %copy.17 = f32[1,3,1024]{2,0,1:T(1,128)} copy(f32[1,3,1024]{2,0,1:T(1,128)} %bitcast.10) | data formatting | bytes 24576

commit v4 on v3

--- a/solution.py
+++ b/solution.py
@@ -28,7 +28,7 @@
 TILES = ATOMS // LANES
 TABLE = ATOMS + 2 * HALO
 UNROLL = 8
-HID_UNROLL = 4
+HID_UNROLL = 16
 FAR_AWAY = 1.0e4
 
 
@@ -238,6 +238,32 @@
             for n in range(number)
         ]
 
+    def radial(layer, tile, pair):
+        sides = [
+            hid[tile, pl.ds(pl.multiple_of((2 * pair + n) * 192 + layer * RAD, RAD), RAD), :]
+            for n in range(2)
+        ]
+        return dot(rad_t[layer], side_by_side(*sides))
+
+    def update_of(layer, t):
+        half = dot(mix_t[layer], side_by_side(scaled_ref[t], scaled_ref[t + 1])) * 0.5
+        return half + half * jnp.tanh(half)
+
+    last_ref[...] = emb_t[...].astype(F32)
+
+    def first_tile(tile, _):
+        def pair(p, acc):
+            field = radial(0, tile, p)
+            for side in range(2):
+                index = jnp.broadcast_to(kind[tile, pl.ds(2 * p + side, 1), :], (8, LANES))
+                far = [lane_gather(last_ref[8 * g : 8 * g + 8, :], index) for g in range(C // 8)]
+                acc = acc + jnp.concatenate(far, axis=0) * field[:, tile_of(side)]
+            return acc
+
+        summed = lax.fori_loop(0, FAN // 2, pair, jnp.zeros((C, LANES), F32), unroll=UNROLL)
+        scaled_ref[tile] = (summed / math.sqrt(FAN)).astype(BF16)
+        return 0
+
     def first_block(i, _):
         block = lax.rem(i + 1, BLOCKS)
         start = pl.multiple_of(block * BLK, BLK)
@@ -250,6 +276,16 @@
 
         @pl.when(i == 2)
         def _():
+            for t in range(2 * HALO // LANES):
+                index = send_list[:, tile_of(t)].astype(F32)
+                for part in range(ATOMS // 256):
+                    local = index - 256.0 * part
+                    inside = jnp.logical_and(local >= 0.0, local < 256.0)
+                    sendhot[t, part * 256 : (part + 1) * 256, :] = one_hot_rows(
+                        jnp.where(inside, local, -1.0), iota_ref[...]
+                    )
+
+            lax.fori_loop(2, 6, first_tile, 0)
             for copy in pos_copies() + img_copies():
                 copy.wait()
             behind = pos[...] - band[0]
@@ -303,33 +339,7 @@
 
     lax.fori_loop(0, BLOCKS, first_block, 0)
 
-    def radial(layer, tile, pair):
-        sides = [
-            hid[tile, pl.ds(pl.multiple_of((2 * pair + n) * 192 + layer * RAD, RAD), RAD), :]
-            for n in range(2)
-        ]
-        return dot(rad_t[layer], side_by_side(*sides))
-
-    def update_of(layer, t):
-        half = dot(mix_t[layer], side_by_side(scaled_ref[t], scaled_ref[t + 1])) * 0.5
-        return half + half * jnp.tanh(half)
-
-    last_ref[...] = emb_t[...].astype(F32)
-
-    def first_tile(tile, _):
-        def pair(p, acc):
-            field = radial(0, tile, p)
-            for side in range(2):
-                index = jnp.broadcast_to(kind[tile, pl.ds(2 * p + side, 1), :], (8, LANES))
-                far = [lane_gather(last_ref[8 * g : 8 * g + 8, :], index) for g in range(C // 8)]
-                acc = acc + jnp.concatenate(far, axis=0) * field[:, tile_of(side)]
-            return acc
-
-        summed = lax.fori_loop(0, FAN // 2, pair, jnp.zeros((C, LANES), F32), unroll=UNROLL)
-        scaled_ref[tile] = (summed / math.sqrt(FAN)).astype(BF16)
-        return 0
-
-    lax.fori_loop(0, TILES, first_tile, 0)
+    lax.fori_loop(6, 10, lambda i, _: first_tile(lax.rem(i, TILES), 0), 0)
     for t in range(0, TILES, 2):
         kinds = jnp.broadcast_to(species[:, t * LANES : (t + 2) * LANES], (16, 2 * LANES))
         own_hot = (kinds == lax.broadcasted_iota(I32, kinds.shape, 0)).astype(F32).astype(BF16)
@@ -337,15 +347,6 @@
         for side in range(2):
             t1[t + side + 2] = h1[:, tile_of(side)]
 
-    for t in range(2 * HALO // LANES):
-        index = send_list[:, tile_of(t)].astype(F32)
-        for part in range(ATOMS // 256):
-            local = index - 256.0 * part
-            inside = jnp.logical_and(local >= 0.0, local < 256.0)
-            sendhot[t, part * 256 : (part + 1) * 256, :] = one_hot_rows(
-                jnp.where(inside, local, -1.0), iota_ref[...]
-            )
-
     def lend(phase, table):
         own = jnp.concatenate([table[2 + t] for t in range(8)], axis=1)
         for side in range(2):
@@ -354,14 +355,8 @@
                 sendh[phase, 2 * side + t] = lent[:, tile_of(t)]
 
     lend(0, t1)
-    back_sq, fore_sq = reduce_wait(0, 2)
-    back_len = jnp.sqrt(back_sq + 1e-06)
-    fore_len = jnp.sqrt(fore_sq + 1e-06)
-    tangent = (pos[...] - band[0]) / back_len + (band[1] - pos[...]) / fore_len
-    tang[...] = tangent
     for copy in h_copies(0, t1):
         copy.start()
-    reduce_start(1, (total(jnp.sum(tangent * tangent, axis=0)),))
 
     def gathered(table, layer, tile, pair):
         hot = side_by_side(
@@ -420,9 +415,14 @@
             at = t + side + 2
             t2[at] = (t1[at].astype(F32) + update[:, tile_of(side)]).astype(BF16)
     lend(1, t2)
-    (tau_sq,) = reduce_wait(1, 1)
     for copy in h_copies(1, t2):
         copy.start()
+    back_sq, fore_sq = reduce_wait(0, 2)
+    back_len = jnp.sqrt(back_sq + 1e-06)
+    fore_len = jnp.sqrt(fore_sq + 1e-06)
+    tangent = (pos[...] - band[0]) / back_len + (band[1] - pos[...]) / fore_len
+    tang[...] = tangent
+    reduce_start(1, (total(jnp.sum(tangent * tangent, axis=0)),))
 
     def force_tile(tile):
         at = pl.multiple_of(tile * LANES, LANES)
@@ -461,6 +461,7 @@
             total(jnp.sum(pull * tangent, axis=0)),
         ),
     )
+    (tau_sq,) = reduce_wait(1, 1)
     energy, along = reduce_wait(2, 2)
     energy_out[...] = energy / (ATOMS * n_atom)
     proj = along / tau_sq
@@ -469,8 +470,13 @@
     )
     climbing = pull - 2.0 * proj * tangent
     is_end = jnp.logical_or(img == 0, img == n_img - 1)
-    band_force = jnp.where(climb[...] == 1, climbing, interior)
+    band_force = jnp.where(climb[0] == 1, climbing, interior)
     out[...] = jnp.where(is_end, pull, band_force)
+
+
+def finish(force, energy, force_out, energy_out):
+    force_out[...] = force[...]
+    energy_out[0] = energy[0, 0]
 
 
 def on_device(
@@ -498,7 +504,7 @@
             jax.ShapeDtypeStruct((3, 1, ATOMS), F32),
             jax.ShapeDtypeStruct((1, 1), F32),
         ),
-        in_specs=[vmem, vmem, vmem, vmem, vmem, vmem, vmem, smem, vmem, vmem, vmem, vmem],
+        in_specs=[vmem, vmem, vmem, vmem, vmem, smem, vmem, smem, vmem, vmem, vmem, vmem],
         out_specs=(vmem, vmem),
         scratch_shapes=[
             pltpu.VMEM((8, TABLE), F32),
@@ -543,7 +549,7 @@
         counts.reshape(1, ATOMS),
         neighbours,
         send_list.reshape(1, 2 * HALO),
-        climb.reshape(1, 1),
+        climb,
         embed,
         ref_energy,
         rad_in,
@@ -551,7 +557,17 @@
         mixing,
         w_energy.reshape(1, C),
     )
-    return result.transpose(1, 0, 2), energy.reshape(1)
+    result, energy = pl.pallas_call(
+        finish,
+        out_shape=(
+            jax.ShapeDtypeStruct((3, 1, ATOMS), F32),
+            jax.ShapeDtypeStruct((1,), F32),
+        ),
+        in_specs=[vmem, smem],
+        out_specs=(vmem, smem),
+        name="finish",
+    )(result, energy)
+    return result.transpose(1, 0, 2), energy
 
 
 def solution(mesh):

time: 47.4 us -> 43.2 us (0.911)
  between operations: 3.05 us -> 1.29 us
  local copies, waits for them, and re-layouts: 1.31 us -> 0 us
  Pallas kernels: 42.8 us -> 41.7 us
    pallas_call x1, Pallas kernels: 42.8 us -> 39.8 us  [on_device(): pl.pallas_call(functools.partial(kernel, n_img, n_atom), out_shape=(jax.S...]
    pallas_call x0 -> x1, Pallas kernels: none -> 1.95 us  [on_device(): pl.pallas_call(finish, out_shape=(jax.ShapeDtypeStruct((3, 1, ATOMS), F32...]
    unnamed x1 -> x0, local copies, waits for them, and re-layouts: 1.31 us -> none
where the time goes in v4:
time: 43.2 us; the launch traced here: 43 us
  Pallas kernels  41.7 us (97%)
  between operations  1.29 us (3%)
    pallas_call x1, Pallas kernels, on_device(): pl.pallas_call(functools.partial(kernel, n_img, n_atom), out_shape=(jax.S...  39.8 us
    pallas_call x1, Pallas kernels, on_device(): pl.pallas_call(finish, out_shape=(jax.ShapeDtypeStruct((3, 1, ATOMS), F32...  1.95 us

profile of v4, /device:TPU:1, one launch (start us, length us, event | category | flops | bytes accessed | tf_op | source)
XLA Modules:
  0.0 43.0 jit_solution(6777008345686759118)
XLA Ops:
  1.3 39.8 %band_step.1 = (f32[3,1,1024]{2,1,0:T(1,128)}, f32[1,1]{1,0:T(1,128)}) custom-call(f32[3,1,1024]{2,1,0:T(1,128)} %bitcast.6, s32[1,1024]{1,0:T(1,128)} %bitcast.7, s32[1,1024]{1,0:T(1,128)} %bitcast.8, s32[16,1024]{1,0:T(8,128)} %neighbours.1, s32[1,512]{1,0:T(1,128)} %bitcast.9, s32[1]{0:T(128)S(6)} %copy.14.climb, bf16[4,128]{1,0:T(4,128)(2,1)} %embed.1, ...), custom_call_target="tpu_custom_call" | custom-call | tf_op jit(solution)/shard_map/band_step/pallas_call | solution.py:501
  41.1 1.9 %finish.1 = (f32[3,1,1024]{2,1,0:T(1,128)}, f32[1]{0:T(128)}) custom-call(f32[3,1,1024]{2,1,0:T(1,128)} %get-tuple-element.6.force, f32[1,1]{1,0:T(1,128)} %get-tuple-element.7.energy), custom_call_target="tpu_custom_call" | custom-call | tf_op jit(solution)/shard_map/finish/pallas_call | solution.py:560

commit v5 on v4

--- a/solution.py
+++ b/solution.py
@@ -27,7 +27,7 @@
 WIN = LANES + 2 * HALO
 TILES = ATOMS // LANES
 TABLE = ATOMS + 2 * HALO
-UNROLL = 8
+DEEP = (3, 7)
 HID_UNROLL = 16
 FAR_AWAY = 1.0e4
 
@@ -61,20 +61,31 @@
 def kernel(
     n_img,
     n_atom,
+    pos_in,
+    species_in,
+    counts_in,
+    neighbours_in,
+    send_list_in,
+    climb,
+    embed_in,
+    ref_energy,
+    rad_in_in,
+    rad_out_in,
+    mixing_in,
+    w_energy_in,
+    out,
+    energy_out,
     pos,
     species,
     counts,
     neighbours,
     send_list,
-    climb,
     embed,
-    ref_energy,
     rad_in,
     rad_out,
     mixing,
     w_energy,
-    out,
-    energy_out,
+    in_sem,
     ptab,
     sendpos,
     band,
@@ -85,15 +96,16 @@
     iota_ref,
     hid,
     w_hid,
+    w_first,
     rad_t,
     mix_t,
     emb_t,
     basis,
-    kind,
+    sp_mask,
     delta,
     rel,
     scaled_ref,
-    last_ref,
+    wide_ref,
     own_ref,
     force,
     tang,
@@ -119,6 +131,32 @@
     img_up = ring(img, 1, n_img)
     img_down = ring(img, n_img - 1, n_img)
 
+    inputs = (
+        (pos_in, pos),
+        (species_in, species),
+        (send_list_in, send_list),
+        (embed_in, embed),
+        (rad_in_in, rad_in),
+        (rad_out_in, rad_out),
+        (mixing_in, mixing),
+        (neighbours_in, neighbours),
+        (counts_in, counts),
+        (w_energy_in, w_energy),
+    )
+    loads = [
+        pltpu.make_async_copy(source, target, in_sem.at[n])
+        for n, (source, target) in enumerate(inputs)
+    ]
+    for load in loads:
+        load.start()
+    low_last = lax.rem(me, n_atom // 2) == 0
+
+    def low_turn(i):
+        return jnp.logical_and(i >= 2, (i == 2) != low_last)
+
+    def high_turn(i):
+        return jnp.logical_and(i >= 2, (i == 2) == low_last)
+
     barrier = pltpu.get_barrier_semaphore()
     for d in range(1, n_atom):
         pl.semaphore_signal(
@@ -126,6 +164,9 @@
         )
     for other in (img_up, img_down):
         pl.semaphore_signal(barrier, inc=1, device_id=(other, me), device_id_type=MESH)
+
+    for load in loads:
+        load.wait()
 
     own_cols = slice(HALO, HALO + ATOMS)
     for comp in range(3):
@@ -150,6 +191,10 @@
     emb = embed[...].astype(F32)
     emb_rows = jnp.concatenate([emb, jnp.zeros((C - SPECIES, C), F32)], axis=0)
     emb_t[...] = emb_rows.T.astype(BF16)
+    first = rad_out[0].astype(F32)
+    w_first[...] = (
+        jnp.concatenate([first * emb[k : k + 1, :] for k in range(SPECIES)], axis=0).T.astype(BF16)
+    )
     lane = lax.broadcasted_iota(I32, (NB, C), 1)
     spread = (lane // FAN == lax.broadcasted_iota(I32, (NB, C), 0)).astype(F32).astype(BF16)
     lane64 = lax.broadcasted_iota(I32, (RAD, C), 1) % FAN
@@ -249,23 +294,28 @@
         half = dot(mix_t[layer], side_by_side(scaled_ref[t], scaled_ref[t + 1])) * 0.5
         return half + half * jnp.tanh(half)
 
-    last_ref[...] = emb_t[...].astype(F32)
-
-    def first_tile(tile, _):
-        def pair(p, acc):
-            field = radial(0, tile, p)
-            for side in range(2):
-                index = jnp.broadcast_to(kind[tile, pl.ds(2 * p + side, 1), :], (8, LANES))
-                far = [lane_gather(last_ref[8 * g : 8 * g + 8, :], index) for g in range(C // 8)]
-                acc = acc + jnp.concatenate(far, axis=0) * field[:, tile_of(side)]
-            return acc
-
-        summed = lax.fori_loop(0, FAN // 2, pair, jnp.zeros((C, LANES), F32), unroll=UNROLL)
-        scaled_ref[tile] = (summed / math.sqrt(FAN)).astype(BF16)
+    def first_sum(block, _):
+        pieces = []
+        for s in range(FAN):
+            unit = side_by_side(
+                *[hid[2 * block + t, s * 192 : s * 192 + RAD, :] for t in range(BLK // LANES)]
+            )
+            for k in range(SPECIES):
+                mask = side_by_side(
+                    *[
+                        jnp.broadcast_to(sp_mask[2 * block + t, k, s : s + 1, :], (16, LANES))
+                        for t in range(BLK // LANES)
+                    ]
+                ).astype(BF16)
+                pieces.append(unit * jnp.concatenate([mask] * (RAD // 16), axis=0))
+        wide = jnp.concatenate([w_first[...]] * FAN, axis=1)
+        scaled = (dot(wide, jnp.concatenate(pieces, axis=0)) / math.sqrt(FAN)).astype(BF16)
+        for t in range(BLK // LANES):
+            scaled_ref[2 * block + t] = scaled[:, tile_of(t)]
         return 0
 
     def first_block(i, _):
-        block = lax.rem(i + 1, BLOCKS)
+        block = jnp.where(low_turn(i), 0, jnp.where(high_turn(i), BLOCKS - 1, i + 1))
         start = pl.multiple_of(block * BLK, BLK)
 
         @pl.when(i == 1)
@@ -285,8 +335,21 @@
                         jnp.where(inside, local, -1.0), iota_ref[...]
                     )
 
-            lax.fori_loop(2, 6, first_tile, 0)
-            for copy in pos_copies() + img_copies():
+            lax.fori_loop(1, 3, first_sum, 0)
+
+        @pl.when(low_turn(i))
+        def _():
+            pos_copies()[1].wait_recv()
+
+        @pl.when(high_turn(i))
+        def _():
+            pos_copies()[0].wait_recv()
+
+        @pl.when(i == 3)
+        def _():
+            for copy in pos_copies():
+                copy.wait_send()
+            for copy in img_copies():
                 copy.wait()
             behind = pos[...] - band[0]
             ahead = band[1] - pos[...]
@@ -324,7 +387,8 @@
                 basis[t, k * FAN : (k + 1) * FAN, :] = jnp.exp(-(shifted * shifted) / 8.0).astype(
                     BF16
                 )
-            kind[tile] = got[3].astype(I32)
+            for k in range(SPECIES):
+                sp_mask[tile, k] = (got[3] == float(k)).astype(F32)
 
         def slot(s, _):
             rows = pl.multiple_of(s * 192, 192)
@@ -339,7 +403,7 @@
 
     lax.fori_loop(0, BLOCKS, first_block, 0)
 
-    lax.fori_loop(6, 10, lambda i, _: first_tile(lax.rem(i, TILES), 0), 0)
+    lax.fori_loop(3, 5, lambda i, _: first_sum(lax.rem(i, BLOCKS), 0), 0)
     for t in range(0, TILES, 2):
         kinds = jnp.broadcast_to(species[:, t * LANES : (t + 2) * LANES], (16, 2 * LANES))
         own_hot = (kinds == lax.broadcasted_iota(I32, kinds.shape, 0)).astype(F32).astype(BF16)
@@ -358,54 +422,66 @@
     for copy in h_copies(0, t1):
         copy.start()
 
-    def gathered(table, layer, tile, pair):
+    def gathered(table, layer, tile, pair, nth):
         hot = side_by_side(
             *[
-                one_hot_rows((rel[tile, pl.ds(2 * pair + n, 1), :] & 255).astype(F32), iota_ref[...])
+                one_hot_rows((rel[tile, 2 * pair + n : 2 * pair + n + 1, :] & 255).astype(F32), iota_ref[...])
                 for n in range(2)
             ]
         )
+        parts = 1 if pair in DEEP else 2
         near = jnp.concatenate(
-            [side_by_side(table[tile + 2 * n], table[tile + 2 * n + 1]) for n in range(2)], axis=0
+            [side_by_side(table[tile + 2 * n], table[tile + 2 * n + 1]) for n in range(parts)],
+            axis=0,
         )
         both = dot(near, hot)
-        fars = both[:C], both[C:]
         field = radial(layer + 1, tile, pair)
         far = []
         for side in range(2):
-            index = jnp.broadcast_to(rel[tile, pl.ds(2 * pair + side, 1), :], (8, LANES))
+            index = jnp.broadcast_to(rel[tile, 2 * pair + side : 2 * pair + side + 1, :], (8, LANES))
             low = index & 127
-            second = (index >> 8) == 1
-            third = (index >> 8) == 2
+            high = index >> 7
             pieces = []
             for g in range(C // 8):
-                rows8 = slice(8 * g, 8 * g + 8)
-                value = jnp.where(second, fars[1][rows8, tile_of(side)], fars[0][rows8, tile_of(side)])
-                pieces.append(jnp.where(third, lane_gather(last_ref[rows8, :], low), value))
+                rows = slice(8 * g, 8 * g + 8)
+                value = both[rows, tile_of(side)]
+                if parts == 2:
+                    later = both[C + 8 * g : C + 8 * g + 8, tile_of(side)]
+                    value = jnp.where(high >= 2, later, value)
+                else:
+                    for n in range(2):
+                        value = jnp.where(high == n + 2, lane_gather(wide_ref[nth + n, rows], low), value)
+                pieces.append(jnp.where(high == 4, lane_gather(wide_ref[nth + 2, rows], low), value))
             far.append(jnp.concatenate(pieces, axis=0))
         return far, field
 
     def tile_loop(table, phase, body):
         def step(i, _):
-            tile = lax.rem(i + 2, TILES)
-
-            @pl.when(i == 4)
+            tile = jnp.where(low_turn(i), 0, jnp.where(high_turn(i), TILES - 2, 2 * i + 2))
+
+            @pl.when(low_turn(i))
             def _():
-                for copy in h_copies(phase, table):
-                    copy.wait()
-
-            last_ref[...] = table[tile + 4].astype(F32)
-            body(tile)
+                h_copies(phase, table)[1].wait_recv()
+
+            @pl.when(high_turn(i))
+            def _():
+                h_copies(phase, table)[0].wait_recv()
+
+            for n in range(4):
+                wide_ref[n] = table[tile + 2 + n].astype(F32)
+            for n in range(2):
+                body(tile + n, n)
             return 0
 
-        lax.fori_loop(0, TILES, step, 0)
-
-    def second_tile(tile):
-        def pair(p, acc):
-            far, field = gathered(t1, 0, tile, p)
-            return acc + (far[0] * field[:, tile_of(0)] + far[1] * field[:, tile_of(1)])
-
-        summed = lax.fori_loop(0, FAN // 2, pair, jnp.zeros((C, LANES), F32), unroll=UNROLL)
+        lax.fori_loop(0, TILES // 2, step, 0)
+        for copy in h_copies(phase, table):
+            copy.wait_send()
+
+    def second_tile(tile, nth):
+        summed = jnp.zeros((C, LANES), F32)
+        for p in range(FAN // 2):
+            far, field = gathered(t1, 0, tile, p, nth)
+            summed = summed + (far[0] * field[:, tile_of(0)] + far[1] * field[:, tile_of(1)])
         scaled_ref[tile] = (summed / math.sqrt(FAN)).astype(BF16)
 
     tile_loop(t1, 0, second_tile)
@@ -424,23 +500,19 @@
     tang[...] = tangent
     reduce_start(1, (total(jnp.sum(tangent * tangent, axis=0)),))
 
-    def force_tile(tile):
+    def force_tile(tile, nth):
         at = pl.multiple_of(tile * LANES, LANES)
-        own_ref[...] = t2[tile + 2].astype(F32)
-
-        def pair(p, acc):
-            far, field = gathered(t2, 1, tile, p)
+        own_ref[nth] = t2[tile + 2].astype(F32)
+
+        parts = [jnp.zeros((8, LANES), F32)] * 3
+        for p in range(FAN // 2):
+            far, field = gathered(t2, 1, tile, p, nth)
             for side in range(2):
-                work = far[side] * field[:, tile_of(side)] * own_ref[...]
+                work = far[side] * field[:, tile_of(side)] * own_ref[nth]
                 strip = jnp.sum(work.reshape(C // 8, 8, LANES), axis=0)
-                acc = tuple(
-                    acc[comp] + strip * delta[comp, tile, pl.ds(2 * p + side, 1), :]
-                    for comp in range(3)
-                )
-            return acc
-
-        zero = jnp.zeros((8, LANES), F32)
-        parts = lax.fori_loop(0, FAN // 2, pair, (zero, zero, zero), unroll=UNROLL)
+                row = 2 * p + side
+                for comp in range(3):
+                    parts[comp] = parts[comp] + strip * delta[comp, tile, row : row + 1, :]
         for comp in range(3):
             force[comp, :, pl.ds(at, LANES)] = jnp.sum(parts[comp], axis=0, keepdims=True) * (
                 1.0 / math.sqrt(C)
@@ -497,6 +569,7 @@
 ):
     vmem = pl.BlockSpec(memory_space=pltpu.VMEM)
     smem = pl.BlockSpec(memory_space=pltpu.SMEM)
+    hbm = pl.BlockSpec(memory_space=pltpu.HBM)
     dma = pltpu.SemaphoreType.DMA
     result, energy = pl.pallas_call(
         functools.partial(kernel, n_img, n_atom),
@@ -504,9 +577,20 @@
             jax.ShapeDtypeStruct((3, 1, ATOMS), F32),
             jax.ShapeDtypeStruct((1, 1), F32),
         ),
-        in_specs=[vmem, vmem, vmem, vmem, vmem, smem, vmem, smem, vmem, vmem, vmem, vmem],
+        in_specs=[hbm, hbm, hbm, hbm, hbm, smem, hbm, smem, hbm, hbm, hbm, hbm],
         out_specs=(vmem, vmem),
         scratch_shapes=[
+            pltpu.VMEM((3, 1, ATOMS), F32),
+            pltpu.VMEM((1, ATOMS), I32),
+            pltpu.VMEM((1, ATOMS), I32),
+            pltpu.VMEM((FAN, ATOMS), I32),
+            pltpu.VMEM((1, 2 * HALO), I32),
+            pltpu.VMEM(embed.shape, BF16),
+            pltpu.VMEM(rad_in.shape, BF16),
+            pltpu.VMEM(rad_out.shape, BF16),
+            pltpu.VMEM(mixing.shape, BF16),
+            pltpu.VMEM((1, C), BF16),
+            dma((10,)),
             pltpu.VMEM((8, TABLE), F32),
             pltpu.VMEM((8, 2 * HALO), F32),
             pltpu.VMEM((2, 3, 1, ATOMS), F32),
@@ -517,16 +601,17 @@
             pltpu.VMEM((256, LANES), BF16),
             pltpu.VMEM((TILES, FAN * 192, LANES), BF16),
             pltpu.VMEM((FAN * 192, C), BF16),
+            pltpu.VMEM((C, 256), BF16),
             pltpu.VMEM((3, C, RAD), BF16),
             pltpu.VMEM((2, C, C), BF16),
             pltpu.VMEM((C, C), BF16),
             pltpu.VMEM((2, C, LANES), BF16),
-            pltpu.VMEM((TILES, FAN, LANES), I32),
+            pltpu.VMEM((TILES, SPECIES, FAN, LANES), F32),
             pltpu.VMEM((3, TILES, FAN, LANES), F32),
             pltpu.VMEM((TILES, FAN, LANES), I32),
             pltpu.VMEM((TILES, C, LANES), BF16),
-            pltpu.VMEM((C, LANES), F32),
-            pltpu.VMEM((C, LANES), F32),
+            pltpu.VMEM((4, C, LANES), F32),
+            pltpu.VMEM((2, C, LANES), F32),
             pltpu.VMEM((3, 1, ATOMS), F32),
             pltpu.VMEM((3, 1, ATOMS), F32),
             pltpu.VMEM((3, n_atom, 1, LANES), F32),

time: 43.2 us -> 39.3 us (0.910)
  Pallas kernels: 41.7 us -> 37.7 us
    pallas_call x1, Pallas kernels: 39.8 us -> 35.8 us  [on_device(): pl.pallas_call(functools.partial(kernel, n_img, n_atom), out_shape=(jax.S...]
where the time goes in v5:
time: 39.3 us; the launch traced here: 39 us
  Pallas kernels  37.7 us (96%)
  between operations  1.29 us (3%)
    pallas_call x1, Pallas kernels, on_device(): pl.pallas_call(functools.partial(kernel, n_img, n_atom), out_shape=(jax.S...  35.8 us
    pallas_call x1, Pallas kernels, on_device(): pl.pallas_call(finish, out_shape=(jax.ShapeDtypeStruct((3, 1, ATOMS), F32...  1.95 us

profile of v5, /device:TPU:1, one launch (start us, length us, event | category | flops | bytes accessed | tf_op | source)
XLA Modules:
  0.0 39.0 jit_solution(14653979651270588247)
XLA Ops:
  1.3 35.8 %band_step.1 = (f32[3,1,1024]{2,1,0:T(1,128)}, f32[1,1]{1,0:T(1,128)}) custom-call(f32[3,1,1024]{2,1,0:T(1,128)} %bitcast.6, s32[1,1024]{1,0:T(1,128)} %bitcast.7, s32[1,1024]{1,0:T(1,128)} %bitcast.8, s32[16,1024]{1,0:T(8,128)} %neighbours_in.1, s32[1,512]{1,0:T(1,128)} %bitcast.9, s32[1]{0:T(128)S(6)} %copy.14.climb, bf16[4,128]{1,0:T(4,128)(2,1)} %embed_in.1, ...), custom_call_target="tpu_custom_call" | custom-call | tf_op jit(solution)/shard_map/band_step/pallas_call | solution.py:574
  37.1 1.9 %finish.1 = (f32[3,1,1024]{2,1,0:T(1,128)}, f32[1]{0:T(128)}) custom-call(f32[3,1,1024]{2,1,0:T(1,128)} %get-tuple-element.6.force, f32[1,1]{1,0:T(1,128)} %get-tuple-element.7.energy), custom_call_target="tpu_custom_call" | custom-call | tf_op jit(solution)/shard_map/finish/pallas_call | solution.py:645

commit v6 on v5

--- a/solution.py
+++ b/solution.py
@@ -52,6 +52,16 @@
 
 def side_by_side(left, right):
     return jnp.concatenate([left, right], axis=1)
+
+
+def far_first(n_atom):
+    chips = n_atom // 4
+
+    def hops(step):
+        along = (step // 2) % chips
+        return min(along, chips - along) + 2 * ((step // 2) // chips)
+
+    return sorted(range(1, n_atom), key=lambda step: (-hops(step), step))
 
 
 def tile_of(lane):
@@ -158,14 +168,14 @@
         return jnp.logical_and(i >= 2, (i == 2) == low_last)
 
     barrier = pltpu.get_barrier_semaphore()
-    for d in range(1, n_atom):
+    for d in far_first(n_atom):
         pl.semaphore_signal(
             barrier, inc=1, device_id=(img, ring(me, d, n_atom)), device_id_type=MESH
         )
     for other in (img_up, img_down):
         pl.semaphore_signal(barrier, inc=1, device_id=(other, me), device_id_type=MESH)
 
-    for load in loads:
+    for load in loads[:3]:
         load.wait()
 
     own_cols = slice(HALO, HALO + ATOMS)
@@ -182,6 +192,9 @@
             source = ptab[:, HALO + w * LANES : HALO + (w + 1) * LANES]
             got = jnp.where(high == w, lane_gather(source, low), got)
         sendpos[:, tile_of(t)] = got
+
+    for load in loads[3:7]:
+        load.wait()
 
     iota_ref[...] = lax.broadcasted_iota(I32, (256, LANES), 0).astype(F32).astype(BF16)
     for layer in range(3):
@@ -207,6 +220,9 @@
             start = s * 192 + layer * RAD
             w_hid[start : start + RAD, :] = jnp.where(lane64 == s, wide, 0.0).astype(BF16)
 
+    for load in loads[7:]:
+        load.wait()
+
     def copy_to(source, target, send, recv, device):
         return pltpu.make_async_remote_copy(
             src_ref=source,
@@ -263,7 +279,7 @@
         for n, value in enumerate(values):
             message = jnp.where(lane_row == n, value, message)
         rbuf[phase, me] = message
-        for d in range(1, n_atom):
+        for d in far_first(n_atom):
             copy_to(
                 rbuf.at[phase, me],
                 rbuf.at[phase, me],

time: 39.3 us -> 39.3 us (level)
  no operation moved by 1% of the time
where the time goes in v6:
time: 39.3 us; the launch traced here: 39 us
  Pallas kernels  37.7 us (96%)
  between operations  1.29 us (3%)
    pallas_call x1, Pallas kernels, on_device(): pl.pallas_call(functools.partial(kernel, n_img, n_atom), out_shape=(jax.S...  35.7 us
    pallas_call x1, Pallas kernels, on_device(): pl.pallas_call(finish, out_shape=(jax.ShapeDtypeStruct((3, 1, ATOMS), F32...  1.95 us

profile of v6, /device:TPU:1, one launch (start us, length us, event | category | flops | bytes accessed | tf_op | source)
XLA Modules:
  0.0 39.0 jit_solution(8921596030441670590)
XLA Ops:
  1.3 35.7 %band_step.1 = (f32[3,1,1024]{2,1,0:T(1,128)}, f32[1,1]{1,0:T(1,128)}) custom-call(f32[3,1,1024]{2,1,0:T(1,128)} %bitcast.6, s32[1,1024]{1,0:T(1,128)} %bitcast.7, s32[1,1024]{1,0:T(1,128)} %bitcast.8, s32[16,1024]{1,0:T(8,128)} %neighbours_in.1, s32[1,512]{1,0:T(1,128)} %bitcast.9, s32[1]{0:T(128)S(6)} %copy.14.climb, bf16[4,128]{1,0:T(4,128)(2,1)} %embed_in.1, ...), custom_call_target="tpu_custom_call" | custom-call | tf_op jit(solution)/shard_map/band_step/pallas_call | solution.py:590
  37.0 1.9 %finish.1 = (f32[3,1,1024]{2,1,0:T(1,128)}, f32[1]{0:T(128)}) custom-call(f32[3,1,1024]{2,1,0:T(1,128)} %get-tuple-element.6.force, f32[1,1]{1,0:T(1,128)} %get-tuple-element.7.energy), custom_call_target="tpu_custom_call" | custom-call | tf_op jit(solution)/shard_map/finish/pallas_call | solution.py:661
